TPU v7x, 128 devices: a whole 4x4x4 slice. The times are simulated.
128 devices in a mesh: dp: 4 (over x_lo, core), expert: 32 (over y, x_hi, z).
Axes of the slice: x: 4 (x_hi: 2, x_lo: 2; x = x_hi * 2 + x_lo), y: 4, z: 4, core: 2. Of those that a mesh axis runs over, the one named last changes fastest.
Arguments:
- hidden_in: bfloat16 [16384, 2048], P(('dp', 'expert')), may hold values from -6 to 6
- attn_gain: float32 [2048], replicated, may hold values from 0.1 to 1.9
- query_key_value_weight: bfloat16 [2048, 2560], P('expert'), may hold values from -0.125 to 0.125
- q_gain: float32 [128], replicated, may hold values from 0.1 to 1.9
- key_norm_gain: float32 [128], replicated, may hold values from 0.1 to 1.9
- w_out: bfloat16 [2048, 2048], P('expert'), may hold values from -0.125 to 0.125
- moe_gain: float32 [2048], replicated, may hold values from 0.1 to 1.9
- w_gate_up: bfloat16 [128, 2048, 1536], P(('dp', 'expert')), may hold values from -0.125 to 0.125
- w_down: bfloat16 [128, 768, 2048], P(('dp', 'expert')), may hold values from -0.21875 to 0.21875
- kv_pool: bfloat16 [32, 2, 128, 2, 128], P('dp'), may hold values from -160 to 160
- page_table: int32 [32], replicated, may hold values from 0 to 31, each once
- suffix_lengths: int32 [4, 4], replicated, may hold values from 1 to 2560, 4096 in all within a row
- request_group: int32 [4, 4], replicated, may hold values from 0 to 1
- expert_ids: int32 [16384, 8], P(('dp', 'expert')), may hold values from 0 to 127, all different within a row; in each aligned block of 128 rows (0 to 127, 128 to 255, ...) at most 12 rows name the same one
- gate_weights: float32 [16384, 8], P(('dp', 'expert')), may hold values from 0.05 to 0.3
Outputs:
- hidden_out: bfloat16 [16384, 2048], P(('dp', 'expert'))
- suffix_cache: bfloat16 [16384, 512], P(('dp', 'expert'))
Inputs may be any that keep to these rules, and one draw needn't show every extreme that they name: page_table holds each pool page once. `suffix_lengths`: each row sums to 4096; the largest of each row is exactly 2560. `expert_ids`: a token's 8 experts differ; among the 128 rows of one device no expert is named more than 12 times, and that many times in some device.
All inputs are finite; a program needn't handle non-finite values.
Results may differ from a plain program's by a relative error of at most 0.01.
The roundings to bfloat16 on the way count: a program that leaves them out, or rounds other values in their place, can miss the bound.
Values may be sent and summed in bfloat16 or wider, within the bound.
A program may use at most 256 MiB of HBM per device.

v0:
```python
import math

import jax
import jax.numpy as jnp
from jax import lax
from jax.sharding import PartitionSpec as P

PREFIX_TOKENS = 2048
PAGE_TOKENS = 128


eps = 1e-06
theta = 1000000.0
floor_value = -1e30


def root_mean_scale(value_rows, gain):
    value_rows = value_rows.astype(jnp.float32)
    return (
        value_rows
        * lax.rsqrt(jnp.mean(value_rows * value_rows, axis=-1, keepdims=True) + eps)
        * gain
    )


def rotary_apply(value_rows, token_positions):
    half = value_rows.shape[-1] // 2
    freqs = theta ** (-jnp.arange(half, dtype=jnp.float32) / half)
    angles = token_positions.astype(jnp.float32)[:, None] * freqs[None, :]
    cosine = jnp.cos(angles)[:, None, :]
    sine = jnp.sin(angles)[:, None, :]
    first = value_rows[..., :half]
    second_split = value_rows[..., half:]
    return jnp.concatenate(
        [first * cosine - second_split * sine, second_split * cosine + first * sine], axis=-1
    )


def layout(lengths_row, index):
    ends = jnp.cumsum(lengths_row)
    starts = ends - lengths_row
    request = jnp.sum((index[:, None] >= ends[None, :]).astype(jnp.int32), axis=1)
    chosen = request[:, None] == jnp.arange(lengths_row.shape[0], dtype=jnp.int32)[None, :]
    offset = index - jnp.sum(jnp.where(chosen, starts[None, :], 0), axis=1)
    return (request, offset, chosen)


def attend(carry, queries, key_rows, value_rows, mask, scale):
    high, total, acc = carry
    scores = (
        jnp.einsum("qkgd,skd->kgqs", queries, key_rows, preferred_element_type=jnp.float32) * scale
    )
    scores = jnp.where(mask[None, None], scores, -jnp.inf)
    new_high = jnp.maximum(high, jnp.max(scores, axis=-1))
    weights = jnp.exp(scores - new_high[..., None])
    scale_factor = jnp.exp(high - new_high)
    total = total * scale_factor + jnp.sum(weights, axis=-1)
    acc = acc * scale_factor[..., None] + jnp.einsum(
        "kgqs,skd->kgqd",
        weights.astype(jnp.bfloat16),
        value_rows,
        preferred_element_type=jnp.float32,
    )
    return (new_high, total, acc)


def expert_rows(rows, gate_up, down):
    both = jnp.dot(rows, gate_up, preferred_element_type=jnp.float32)
    half = both.shape[1] // 2
    act = (jax.nn.silu(both[:, :half]) * both[:, half:]).astype(jnp.bfloat16)
    return jnp.dot(act, down, preferred_element_type=jnp.float32).astype(jnp.bfloat16)


def local(
    hidden_in,
    attn_gain,
    query_key_value_weight,
    q_gain,
    key_norm_gain,
    w_out,
    moe_gain,
    w_gate_up,
    w_down,
    kv_pool,
    page_table,
    suffix_lengths,
    request_group,
    expert_ids,
    gate_weights,
):
    tokens_here, width = hidden_in.shape
    page_rows = kv_pool.shape[2]
    kv_heads = kv_pool.shape[3]
    head_dim = kv_pool.shape[4]
    key_value_width = kv_heads * head_dim
    query_width = query_key_value_weight.shape[1] - 2 * key_value_width
    q_heads = query_width // head_dim
    head_split = q_heads // kv_heads
    scale = 1.0 / math.sqrt(head_dim)
    row_count = lax.axis_size("dp")
    col_count = lax.axis_size("expert")
    row = lax.axis_index("dp")
    col = lax.axis_index("expert")
    normed = root_mean_scale(hidden_in, attn_gain).astype(jnp.bfloat16)
    part = normed
    qkv = jnp.dot(
        part,
        lax.all_gather(query_key_value_weight, "expert", axis=0, tiled=True),
        preferred_element_type=jnp.float32,
    )
    index = col * tokens_here + jnp.arange(tokens_here, dtype=jnp.int32)
    lengths_row = lax.dynamic_index_in_dim(suffix_lengths, row, 0, keepdims=False)
    groups_row = lax.dynamic_index_in_dim(request_group, row, 0, keepdims=False)
    request, offset, chosen = layout(lengths_row, index)
    qgroup = jnp.sum(jnp.where(chosen, groups_row[None, :], 0), axis=1)
    token_positions = PREFIX_TOKENS + offset
    queries = rotary_apply(
        root_mean_scale(qkv[:, :query_width].reshape(tokens_here, q_heads, head_dim), q_gain),
        token_positions,
    ).astype(jnp.bfloat16)
    key_rows = rotary_apply(
        root_mean_scale(
            qkv[:, query_width : query_width + key_value_width].reshape(
                tokens_here, kv_heads, head_dim
            ),
            key_norm_gain,
        ),
        token_positions,
    ).astype(jnp.bfloat16)
    value_rows = (
        qkv[:, query_width + key_value_width :]
        .reshape(tokens_here, kv_heads, head_dim)
        .astype(jnp.bfloat16)
    )
    suffix_cache = jnp.concatenate(
        [
            key_rows.reshape(tokens_here, key_value_width),
            value_rows.reshape(tokens_here, key_value_width),
        ],
        axis=1,
    )
    grouped = queries.reshape(tokens_here, kv_heads, head_split, head_dim)
    carry = (
        jnp.full((kv_heads, head_split, tokens_here), floor_value, jnp.float32),
        jnp.zeros((kv_heads, head_split, tokens_here), jnp.float32),
        jnp.zeros((kv_heads, head_split, tokens_here, head_dim), jnp.float32),
    )
    piece_keys = lax.all_gather(key_rows, "expert", axis=0, tiled=True)
    piece_values = lax.all_gather(value_rows, "expert", axis=0, tiled=True)
    key_index = jnp.arange(piece_keys.shape[0], dtype=jnp.int32)
    key_request, _, _ = layout(lengths_row, key_index)
    mask = (key_request[None, :] == request[:, None]) & (key_index[None, :] <= index[:, None])
    carry = attend(carry, grouped, piece_keys, piece_values, mask, scale)
    per_group = PREFIX_TOKENS // PAGE_TOKENS
    slot_ids = jnp.arange(page_table.shape[0], dtype=jnp.int32)
    piece = lax.all_gather(kv_pool, "dp", axis=0, tiled=True)
    count = piece.shape[0]
    hit = page_table[None, :] == jnp.arange(count, dtype=jnp.int32)[:, None]
    key_group = jnp.repeat(
        jnp.sum(jnp.where(hit, slot_ids[None, :] // per_group, 0), axis=1), page_rows
    )
    mask = key_group[None, :] == qgroup[:, None]
    carry = attend(
        carry,
        grouped,
        piece[:, 0].reshape(count * page_rows, kv_heads, head_dim),
        piece[:, 1].reshape(count * page_rows, kv_heads, head_dim),
        mask,
        scale,
    )
    mixed = (
        (carry[2] / carry[1][..., None])
        .transpose(2, 0, 1, 3)
        .reshape(tokens_here, query_width)
        .astype(jnp.bfloat16)
    )
    part = mixed
    projected = jnp.dot(
        part,
        lax.all_gather(w_out, "expert", axis=0, tiled=True),
        preferred_element_type=jnp.float32,
    )
    mid = (hidden_in.astype(jnp.float32) + projected).astype(jnp.bfloat16)
    moe_in = root_mean_scale(mid, moe_gain).astype(jnp.bfloat16)
    top_k = expert_ids.shape[1]
    expert_count = row_count * col_count
    capacity = max(2, tokens_here * top_k * 3 // (2 * expert_count))
    flat = expert_ids.reshape(-1)
    onehot = (flat[:, None] == jnp.arange(expert_count, dtype=jnp.int32)[None, :]).astype(jnp.int32)
    slot = jnp.sum((jnp.cumsum(onehot, axis=0) - onehot) * onehot, axis=1)
    place = flat * capacity + slot
    sources = jnp.repeat(moe_in, top_k, axis=0)
    outgoing = jnp.zeros((expert_count * capacity, width), jnp.bfloat16).at[place].set(sources)
    gate_up = w_gate_up[0]
    down = w_down[0]
    received = lax.all_to_all(
        outgoing.reshape(expert_count, capacity, width),
        ("dp", "expert"),
        split_axis=0,
        concat_axis=0,
        tiled=True,
    )
    results = expert_rows(received.reshape(-1, width), gate_up, down).reshape(received.shape)
    returned = lax.all_to_all(results, ("dp", "expert"), split_axis=0, concat_axis=0, tiled=True)
    picked = returned.reshape(expert_count * capacity, width)[place].astype(jnp.float32)
    moe = jnp.sum(picked.reshape(tokens_here, top_k, width) * gate_weights[:, :, None], axis=1)
    hidden_out = (mid.astype(jnp.float32) + moe).astype(jnp.bfloat16)
    return (hidden_out, suffix_cache)


def solution(mesh):
    return jax.shard_map(
        local,
        mesh=mesh,
        in_specs=(
            P(("dp", "expert"), None),
            P(),
            P("expert", None),
            P(),
            P(),
            P("expert", None),
            P(),
            P(("dp", "expert"), None, None),
            P(("dp", "expert"), None, None),
            P("dp", None, None, None, None),
            P(),
            P(),
            P(),
            P(("dp", "expert"), None),
            P(("dp", "expert"), None),
        ),
        out_specs=(P(("dp", "expert"), None), P(("dp", "expert"), None)),
        check_vma=False,
    )
```

profile of v0, /device:TPU:1, one launch (start us, length us, event | category | flops | bytes accessed | tf_op | source)
XLA Modules:
  0.0 754.0 jit_solution(2184994517330569896)
XLA Ops:
  7.2 0.7 all-gather.6.cloned.1.call-update
  8.0 2.6 copy.97
  10.7 0.7 fusion.84
  11.6 0.7 fusion.83
  12.4 1.2 fusion.65
  13.7 0.3 multiply_cosine_fusion
  14.0 117.0 %all-gather.6.cloned.1.call-done = bf16[2048,2560]{1,0:T(8,128)(2,1)} async-done(((bf16[64,2560]{1,0:T(8,128)(2,1)}), bf16[2048,2560]{1,0:T(8,128)(2,1)}) %all-gather.6.cloned.1.call-update) | async-done | bytes 10485776 | tf_op jit(solution)/shard_map/all_gather | solution.py:108
  131.0 5.7 fusion.68
  136.8 1.1 copy-done.8
  137.8 0.7 fusion.95
  138.5 1.6 reshape.345
  140.1 1.1 multiply_reduce_fusion.2
  141.6 0.6 copy-done.12
  142.2 0.7 maximum_convert_fusion
  143.0 0.9 slice.85
  144.0 0.7 copy.112
  144.8 0.5 all-gather.14.cloned.1.call-update
  145.7 0.2 fusion.72
  146.0 0.8 copy-done.11
  146.8 1.9 broadcast_add_fusion
  148.9 1.9 copy.104
  151.0 1.4 fusion.71
  152.5 1.2 broadcast_compare_fusion
  153.7 3.1 fusion.29
  156.8 21.2 %all-gather.12.cloned.1.call-done = bf16[32,2,128,2,128]{4,2,3,1,0:T(8,128)(2,1)} async-done(((bf16[8,2,128,2,128]{4,2,3,1,0:T(8,128)(2,1)}), bf16[32,2,128,2,128]{4,2,3,1,0:T(8,128)(2,1)}) %all-gather.12.cloned.1.call-update) | async-done | bytes 4194320 | tf_op jit(solution)/shard_map/all_gather | solution.py:156
  178.0 4.1 fusion.94
  182.0 1.6 copy.98
  183.6 4.6 copy.99
  188.3 4.2 reshape.374
  192.5 1.3 slice_bitcast_fusion
  193.8 0.2 copy.115
  194.0 1.0 copy-done.6
  195.0 0.3 multiply_reduce_fusion.1
  195.6 1.7 multiply_multiply_fusion
  197.3 0.5 subtract_convert_fusion
  198.1 0.6 copy-done.9
  198.8 0.2 copy-done.10
  199.0 13.7 %bitcast_reduce_fusion = (f32[2,8,128]{2,1,0:T(8,128)S(1)}, f32[2,128,8,4096]{3,1,2,0:T(8,128)}) fusion(pred[128,4096]{1,0:T(8,128)(4,1)S(1)} %copy-done.2, bf16[4096,2,128,1]{2,0,3,1:T(8,128)(2,1)S(1)} %bitcast.168, bf16[128,2,8,64]{3,0,2,1:T(8,128)(2,1)S(1)} %bitcast.171, bf16[128,2,8,64]{3,0,2,1:T(8,128)(2,1)S(1)} %bitcast.169), kind=kOutput, calls=%fused_computation.3 | convolution fusion | flops 2173696000 | bytes 36708352 | tf_op jit(solution)/shard_map/qkgd,skd->kgqs/dot_general | solution.py:51
  212.6 39.2 %all-gather.8.cloned.1.call-done = bf16[4096,2,128]{2,0,1:T(8,128)(2,1)} async-done(((bf16[128,2,128]{2,0,1:T(8,128)(2,1)}), bf16[4096,2,128]{2,0,1:T(8,128)(2,1)}) %all-gather.8.cloned.1.call-update) | async-done | bytes 2097168 | tf_op jit(solution)/shard_map/all_gather | solution.py:148
  251.9 15.0 %fusion.3 = (f32[2,8,128]{2,1,0:T(8,128)S(1)}, f32[2,4096,128,8]{2,1,3,0:T(8,128)}) fusion(pred[128,4096]{0,1:T(8,128)(4,1)} %fusion.29, bf16[128,2,8,64]{3,0,2,1:T(8,128)(2,1)} %bitcast.172, bf16[128,2,8,64]{3,0,2,1:T(8,128)(2,1)} %bitcast.170, bf16[4096,2,128]{2,0,1:T(8,128)(2,1)} %all-gather.8.cloned.1.call-done), kind=kOutput, calls=%fused_computation.10 | convolution fusion | flops 2173696000 | bytes 36708352 | tf_op jit(solution)/shard_map/qkgd,skd->kgqs/dot_general | solution.py:51
  266.8 16.4 %fusion.1 = f32[2,8,128]{2,1,0:T(8,128)S(1)} fusion(f32[2,4096,128,8]{2,1,3,0:T(8,128)} %get-tuple-element.22, f32[2,8,128]{2,1,0:T(8,128)S(1)} %get-tuple-element.16, pred[128,4096]{0,1:T(8,128)(4,1)S(1)} %copy-done.4), kind=kLoop, calls=%fused_computation.8 | loop fusion | flops 33552384 | bytes 34095104 | tf_op jit(solution)/shard_map/reduce_sum | solution.py:57
  283.3 3.8 copy-done.1
  287.1 9.5 %fusion.4 = f32[2,8,128]{2,1,0:T(8,128)S(1)} fusion(f32[2,128,8,4096]{3,1,2,0:T(8,128)S(1)} %copy-done.1, f32[2,8,128]{2,1,0:T(8,128)S(1)} %get-tuple-element.15, pred[128,4096]{1,0:T(8,128)(4,1)S(1)} %copy-done.3), kind=kLoop, calls=%fused_computation.11 | loop fusion | flops 33552384 | bytes 34095104 | tf_op jit(solution)/shard_map/reduce_sum | solution.py:57
  296.7 30.2 %all-gather.10.cloned.1.call-done = bf16[4096,2,128]{0,2,1:T(8,128)(2,1)} async-done(((bf16[128,2,128]{0,2,1:T(8,128)(2,1)}), bf16[4096,2,128]{0,2,1:T(8,128)(2,1)}) %all-gather.10.cloned.1.call-update) | async-done | bytes 2097168 | tf_op jit(solution)/shard_map/all_gather | solution.py:149
  326.8 16.3 %fusion.50 = f32[128,2,8,128]{0,3,2,1:T(8,128)} fusion(f32[2,4096,128,8]{2,1,3,0:T(8,128)} %get-tuple-element.22, f32[2,8,128]{2,1,0:T(8,128)S(1)} %get-tuple-element.16, pred[128,4096]{0,1:T(8,128)(4,1)} %fusion.29, bf16[4096,2,128]{0,2,1:T(8,128)(2,1)} %all-gather.10.cloned.1.call-done, f32[128,2,8]{0,2,1:T(8,128)S(1)} %get-tuple-element.5, ...), kind=kOutput, calls=%fused_computation.45 | convolution fusion | flops 2181562368 | bytes 37249024 | tf_op jit(solution)/shard_map/kgqs,skd->kgqd/dot_general | solution.py:58
  343.2 16.3 %fusion.60 = bf16[128,2,8,128]{0,3,2,1:T(8,128)(2,1)} fusion(f32[128,2,8,128]{0,3,2,1:T(8,128)} %fusion.50, bf16[4096,2,128,1]{0,2,1,3:T(8,128)(2,1)} %reshape.374, f32[2,128,8,4096]{3,1,2,0:T(8,128)} %get-tuple-element.20, f32[2,8,128]{2,1,0:T(8,128)S(1)} %get-tuple-element.15, pred[128,4096]{1,0:T(8,128)(4,1)} %broadcast_compare_fusion, ...), kind=kOutput, calls=%fused_computation.47 | convolution fusion | flops 2181824512 | bytes 37765120 | tf_op jit(solution)/shard_map/kgqs,skd->kgqd/dot_general | solution.py:58
  359.5 72.0 %all-gather.14.cloned.1.call-done = bf16[2048,2048]{1,0:T(8,128)(2,1)} async-done(((bf16[64,2048]{1,0:T(8,128)(2,1)}), bf16[2048,2048]{1,0:T(8,128)(2,1)}) %all-gather.14.cloned.1.call-update) | async-done | bytes 8388624 | tf_op jit(solution)/shard_map/all_gather | solution.py:180
  431.4 4.9 multiply_reduce_fusion
  436.4 1.0 copy-done.5
  437.4 0.9 multiply_convert_fusion
  438.3 10.9 %scatter_custom_fusion = bf16[1536,2048]{1,0:T(8,128)(2,1)} fusion(s32[1024]{0:T(1024)S(1)} %bitcast.176, bf16[]{:T(256)} %constant.80.clone.1, bf16[128,2048]{1,0:T(8,128)(2,1)} %multiply_convert_fusion), kind=kCustom, calls=%fused_computation.24 | custom fusion | bytes 6815746 | tf_op jit(solution)/shard_map/scatter | solution.py:193
  449.3 10.6 %reshape.350 = bf16[128,12,2048]{2,1,0:T(8,128)(2,1)} reshape(bf16[1536,2048]{1,0:T(8,128)(2,1)} %scatter_custom_fusion) | data formatting | bytes 12582912 | tf_op jit(solution)/shard_map/reshape | solution.py:197
  459.9 104.4 %all_to_all.10 = bf16[128,12,2048]{2,1,0:T(8,128)(2,1)} all-to-all(bf16[128,12,2048]{2,1,0:T(8,128)(2,1)} %reshape.350), channel_id=1, replica_groups=mesh['dp'=4,'expert'=32] {'dp','expert'}, dimensions={0} | all-to-all | bytes 12582912 | tf_op jit(solution)/shard_map/all_to_all | solution.py:196
  564.2 10.7 %reshape.351 = bf16[1536,2048]{1,0:T(8,128)(2,1)} reshape(bf16[128,12,2048]{2,1,0:T(8,128)(2,1)} %all_to_all.10) | data formatting | bytes 12582912 | tf_op jit(solution)/shard_map/reshape | solution.py:203
  574.9 14.1 %fusion.13 = f32[1536,1536]{1,0:T(8,128)S(1)} fusion(bf16[1536,2048]{1,0:T(8,128)(2,1)} %reshape.351, bf16[1,2048,1536]{2,1,0:T(8,128)(2,1)} %param.22), kind=kOutput, calls=%fused_computation.20 | convolution fusion | flops 9663676416 | bytes 22020096 | tf_op jit(solution)/shard_map/dot_general | solution.py:68
  589.1 7.1 convolution_convert_fusion
  596.2 10.6 %reshape.352 = bf16[128,12,2048]{2,1,0:T(8,128)(2,1)} reshape(bf16[1536,2048]{1,0:T(8,128)(2,1)} %convolution_convert_fusion) | data formatting | bytes 12582912 | tf_op jit(solution)/shard_map/reshape | solution.py:203
  606.7 6.8 all-to-all-start.1
  613.8 0.7 pad_maximum_fusion.1
  614.5 100.8 %all-to-all-done.1 = bf16[128,12,2048]{2,1,0:T(8,128)(2,1)} async-done(((bf16[128,12,2048]{2,1,0:T(8,128)(2,1)}), bf16[128,12,2048]{2,1,0:T(8,128)(2,1)}, u32[]{:S(2)}, u32[]{:S(2)}) %all-to-all-start.1) | async-done | bytes 6291488 | tf_op jit(solution)/shard_map/all_to_all | solution.py:204
  715.3 10.7 %reshape.353 = bf16[1536,2048]{1,0:T(8,128)(2,1)} reshape(bf16[128,12,2048]{2,1,0:T(8,128)(2,1)} %all-to-all-done.1) | data formatting | bytes 12582912 | tf_op jit(solution)/shard_map/reshape | solution.py:205
  726.0 12.4 %gather_fusion = bf16[1024,2048]{1,0:T(8,128)(2,1)} fusion(bf16[1536,2048]{1,0:T(8,128)(2,1)} %reshape.353, s32[1024]{0:T(1024)S(1)} %broadcast_clamp_fusion), kind=kCustom, calls=%fused_computation | custom fusion | bytes 8392704 | tf_op jit(solution)/shard_map/gather | solution.py:205
  738.5 6.5 fusion.12
  745.0 2.2 add_convert_fusion
  (85 shorter events, 2.7 us)
Async XLA Ops:
  7.2 581.9 %copy-start = (bf16[1,768,2048]{2,1,0:T(8,128)(2,1)S(1)}, bf16[1,768,2048]{2,1,0:T(8,128)(2,1)}, u32[]{:S(2)}) copy-start(bf16[1,768,2048]{2,1,0:T(8,128)(2,1)} %param.23) | copy-start | bytes 9437188
  7.2 123.8 %all-gather.6.cloned.1.call-start = ((), (), s32[]{:S(2)}) async-start(), calls=%async_computation.2 | async-start | bytes 10813440 | tf_op jit(solution)/shard_map/all_gather | solution.py:108
  7.9 170.1 %all-gather.12.cloned.1.call-start = ((), (), s32[]{:S(2)}) async-start(), calls=%async_computation.5 | async-start | bytes 5242880 | tf_op jit(solution)/shard_map/all_gather | solution.py:156
  10.6 241.3 %all-gather.8.cloned.1.call-start = ((), (), s32[]{:S(2)}) async-start(), calls=%async_computation.3 | async-start | bytes 2162688 | tf_op jit(solution)/shard_map/all_gather | solution.py:148
  14.0 127.4 %copy-start.21 = (f32[128]{0:T(128)S(1)}, f32[128]{0:T(128)}, u32[]{:S(2)}) copy-start(f32[128]{0:T(128)} %param.19) | copy-start | bytes 1540
  14.0 131.4 %copy-start.18 = (s32[128,8]{0,1:T(8,128)S(1)}, s32[128,8]{0,1:T(8,128)}, u32[]{:S(2)}) copy-start(s32[128,8]{0,1:T(8,128)} %param.28) | copy-start | bytes 12292
  14.0 134.7 %copy-start.23 = (s32[32]{0:T(128)S(1)}, s32[32]{0:T(128)}, u32[]{:S(2)}) copy-start(s32[32]{0:T(128)} %param.25) | copy-start | bytes 388
  136.7 1.1 copy-start.8
  141.6 0.6 copy-start.12
  141.6 0.6 copy-start.14
  143.0 183.8 %all-gather.10.cloned.1.call-start = ((), (), s32[]{:S(2)}) async-start(), calls=%async_computation.4 | async-start | bytes 2162688 | tf_op jit(solution)/shard_map/all_gather | solution.py:149
  144.0 1.4 copy-start.16
  144.7 286.7 %all-gather.14.cloned.1.call-start = ((), (), s32[]{:S(2)}) async-start(), calls=%async_computation.6 | async-start | bytes 8650752 | tf_op jit(solution)/shard_map/all_gather | solution.py:180
  146.0 0.8 copy-start.11
  182.0 13.5 %copy-start.22 = (f32[128]{0:T(128)S(1)}, f32[128]{0:T(128)}, u32[]{:S(2)}) copy-start(f32[128]{0:T(128)} %param.18) | copy-start | bytes 1540
  194.0 1.0 copy-start.6
  195.5 3.4 copy-start.2
  195.5 3.4 copy-start.7
  198.0 0.8 copy-start.9
  198.1 0.9 copy-start.10
  251.9 15.0 %copy-start.4 = (pred[128,4096]{0,1:T(8,128)(4,1)S(1)}, pred[128,4096]{0,1:T(8,128)(4,1)}, u32[]{:S(2)}) copy-start(pred[128,4096]{0,1:T(8,128)(4,1)} %fusion.29) | copy-start | bytes 1572868
  266.8 20.3 %copy-start.1 = (f32[2,128,8,4096]{3,1,2,0:T(8,128)S(1)}, f32[2,128,8,4096]{3,1,2,0:T(8,128)}, u32[]{:S(2)}) copy-start(f32[2,128,8,4096]{3,1,2,0:T(8,128)} %get-tuple-element.20) | copy-start | bytes 100663296
  266.8 20.3 %copy-start.3 = (pred[128,4096]{1,0:T(8,128)(4,1)S(1)}, pred[128,4096]{1,0:T(8,128)(4,1)}, u32[]{:S(2)}) copy-start(pred[128,4096]{1,0:T(8,128)(4,1)} %broadcast_compare_fusion) | copy-start | bytes 1572868
  431.4 6.0 copy-start.19
  436.4 1.0 copy-start.5
  606.7 6.8 copy-start.20
  606.7 7.0 copy-start.13
  606.7 7.0 copy-start.15
  606.7 7.1 copy-start.17
  606.7 108.6 %all-to-all-start.1 = ((bf16[128,12,2048]{2,1,0:T(8,128)(2,1)}), bf16[128,12,2048]{2,1,0:T(8,128)(2,1)}, u32[]{:S(2)}, u32[]{:S(2)}) async-start(bf16[128,12,2048]{2,1,0:T(8,128)(2,1)} %reshape.352), calls=%async_computation.1 | async-start | bytes 16777216 | tf_op jit(solution)/shard_map/all_to_all | solution.py:204
Sparse Core Ops, SparseCore 0:
  11.1 119.8 all-gather.5
  132.7 45.2 all-gather.11
  181.8 70.0 all-gather.7
  254.5 72.3 all-gather.9
  329.7 101.6 all-gather.13
where the time goes:
time: 762 us; the launch traced here: 754 us
  waiting for transfers between devices  382 us (50%)
  blocking collectives  104 us (14%)
  local copies, waits for them, and re-layouts  102 us (13%)
  matrix products  93.2 us (12%)
  other arithmetic  51.6 us (7%)
  between operations  14.5 us (2%)
    all_gather x1, waiting for transfers between devices, local(): lax.all_gather(query_key_value_weight, 'expert', axis=0, tiled=True)  117 us
    all_to_all x1, blocking collectives, local(): lax.all_to_all(outgoing.reshape(expert_count, capacity, width), ('dp', 'e...  104 us
    all_to_all x1, waiting for transfers between devices, local(): lax.all_to_all(results, ('dp', 'expert'), split_axis=0, concat_axis=0, ti...  101 us
    all_gather x1, waiting for transfers between devices, local(): lax.all_gather(w_out, 'expert', axis=0, tiled=True)  72 us
    all_gather x1, waiting for transfers between devices, local(): piece_keys = lax.all_gather(key_rows, 'expert', axis=0, tiled=True)  39.2 us
    dot_general x2, matrix products, attend(): jnp.einsum('kgqs,skd->kgqd', weights.astype(jnp.bfloat16), value_rows, pr...  32.7 us
    all_gather x1, waiting for transfers between devices, local(): piece_values = lax.all_gather(value_rows, 'expert', axis=0, tiled=True)  30.2 us
    dot_general x2, matrix products, attend(): jnp.einsum('qkgd,skd->kgqs', queries, key_rows, preferred_element_type=jn...  28.6 us
  transfers between devices with their start and end apart: 6, of which 6 were waited for; matrix products, arithmetic and copies ran while one was open for 18% of the time, Pallas kernels for 0%

commit v1 on v0

--- a/solution.py
+++ b/solution.py
@@ -3,6 +3,8 @@
 import jax
 import jax.numpy as jnp
 from jax import lax
+from jax.experimental import pallas as pl
+from jax.experimental.pallas import tpu as pltpu
 from jax.sharding import PartitionSpec as P
 
 PREFIX_TOKENS = 2048
@@ -64,11 +66,311 @@
     return (new_high, total, acc)
 
 
-def expert_rows(rows, gate_up, down):
-    both = jnp.dot(rows, gate_up, preferred_element_type=jnp.float32)
-    half = both.shape[1] // 2
-    act = (jax.nn.silu(both[:, :half]) * both[:, half:]).astype(jnp.bfloat16)
-    return jnp.dot(act, down, preferred_element_type=jnp.float32).astype(jnp.bfloat16)
+MESH_ID = pl.DeviceIdType.MESH
+STEP = 45
+CHUNK = 16
+
+
+def place():
+    dp = lax.axis_index("dp")
+    ex = lax.axis_index("expert")
+    x = lax.rem(lax.div(ex, 4), 2) * 2 + lax.div(dp, 2)
+    return (x, lax.div(ex, 8), lax.rem(ex, 4), lax.rem(dp, 2))
+
+
+def device(x, y, z, c):
+    return {"dp": lax.rem(x, 2) * 2 + c, "expert": y * 8 + lax.div(x, 2) * 4 + z}
+
+
+def number(x, y, z, c):
+    return (lax.rem(x, 2) * 2 + c) * 32 + y * 8 + lax.div(x, 2) * 4 + z
+
+
+def shift(k):
+    o = lax.rem(k * STEP, 128)
+    return (lax.div(o, 32), lax.rem(lax.div(o, 8), 4), lax.rem(lax.div(o, 2), 4), lax.rem(o, 2))
+
+
+def target(here, k):
+    x, y, z, c = here
+    dx, dy, dz, dc = shift(k)
+    sign = 1 - 2 * c
+    return (
+        lax.rem(x + sign * dx + 4, 4),
+        lax.rem(y + sign * dy + 4, 4),
+        lax.rem(z + sign * dz + 4, 4),
+        lax.rem(c + dc, 2),
+    )
+
+
+def origin(here, k):
+    x, y, z, c = here
+    dx, dy, dz, dc = shift(k)
+    source_core = lax.rem(c + dc, 2)
+    sign = 1 - 2 * source_core
+    return (
+        lax.rem(x - sign * dx + 4, 4),
+        lax.rem(y - sign * dy + 4, 4),
+        lax.rem(z - sign * dz + 4, 4),
+        source_core,
+    )
+
+
+def greet_all(here):
+    barrier = pltpu.get_barrier_semaphore()
+
+    def tell(k, _):
+        pl.semaphore_signal(
+            barrier, inc=1, device_id=device(*target(here, k)), device_id_type=MESH_ID
+        )
+        return 0
+
+    lax.fori_loop(1, 128, tell, 0)
+    return barrier
+
+
+def send(src, dst, send_sem, recv_sem, where):
+    return pltpu.make_async_remote_copy(
+        src_ref=src,
+        dst_ref=dst,
+        send_sem=send_sem,
+        recv_sem=recv_sem,
+        device_id=device(*where),
+        device_id_type=MESH_ID,
+    )
+
+
+def moe_kernel(
+    x_ref,
+    ids_ref,
+    gates_ref,
+    gate_up_hbm,
+    down_hbm,
+    out_ref,
+    send_a,
+    send_b,
+    recv_a,
+    recv_b,
+    back_a,
+    back_b,
+    home_a,
+    home_b,
+    gate_up,
+    down,
+    rows,
+    acts,
+    result,
+    rank_ref,
+    gate_ref,
+    weight_sem,
+    out_sem,
+    in_a_sem,
+    in_b_sem,
+    back_sem,
+    home_sem,
+):
+    f32, bf16 = jnp.float32, jnp.bfloat16
+    width = x_ref.shape[1]
+    half = width // 2
+    ff = down.shape[0]
+    here = place()
+    me = number(*here)
+    load_gate_up = pltpu.make_async_copy(gate_up_hbm, gate_up, weight_sem.at[0])
+    load_down = pltpu.make_async_copy(down_hbm, down, weight_sem.at[1])
+    load_gate_up.start()
+    load_down.start()
+    barrier = greet_all(here)
+
+    expert = lax.broadcasted_iota(jnp.int32, (128, 128), 0)
+    token = lax.broadcasted_iota(jnp.int32, (128, 128), 1)
+    named = jnp.zeros((128, 128), f32)
+    gates = jnp.zeros((128, 128), f32)
+    for k in range(ids_ref.shape[0]):
+        hit = ids_ref[k : k + 1, :] == expert
+        named += jnp.where(hit, 1.0, 0.0)
+        gates += jnp.where(hit, gates_ref[k : k + 1, :], 0.0)
+    before = jnp.where(expert < token, 1.0, 0.0).astype(bf16)
+    rank = jnp.dot(named.astype(bf16), before, preferred_element_type=f32)
+    rank_ref[...] = jnp.where(named > 0.5, rank, -1.0)
+    gate_ref[...] = gates
+
+    slot = lax.broadcasted_iota(jnp.int32, (32, 8, 128), 1)
+
+    def choice(part, wanted):
+        ranks = rank_ref[pl.ds(part * 32, 32), :]
+        return jnp.where(ranks[:, None, :] == wanted.astype(f32), 1.0, 0.0)
+
+    def pack(part, _):
+        first = choice(part, slot).reshape(256, 128).astype(bf16)
+        send_a[pl.ds(part * 256, 256), :] = jnp.dot(
+            first, x_ref[...], preferred_element_type=f32
+        ).astype(bf16)
+        low = choice(part, jnp.where(slot < 4, slot + 8, 99)).reshape(256, 128).astype(bf16)
+        high = choice(part, jnp.where(slot >= 4, slot + 4, 99)).reshape(256, 128).astype(bf16)
+        mixed = jnp.dot(low, x_ref[:, :half], preferred_element_type=f32)
+        mixed += jnp.dot(high, x_ref[:, half:], preferred_element_type=f32)
+        send_b[pl.ds(part * 256, 256), :] = mixed.astype(bf16)
+        return 0
+
+    lax.fori_loop(0, 4, pack, 0)
+    pl.semaphore_wait(barrier, 127)
+
+    def piece(ref, index):
+        return ref.at[pl.ds(index * 8, 8), :]
+
+    def dispatch(k, _):
+        there = target(here, k)
+        to = number(*there)
+        group = lax.div(k, CHUNK)
+        send(piece(send_a, to), piece(recv_a, k), out_sem.at[0], in_a_sem.at[group], there).start()
+        send(piece(send_b, to), piece(recv_b, k), out_sem.at[1], in_b_sem.at[group], there).start()
+        return 0
+
+    own_a = pltpu.make_async_copy(piece(send_a, me), piece(recv_a, 0), in_a_sem.at[0])
+    own_b = pltpu.make_async_copy(piece(send_b, me), piece(recv_b, 0), in_b_sem.at[0])
+    own_a.start()
+    own_b.start()
+    lax.fori_loop(1, 128, dispatch, 0)
+    load_gate_up.wait()
+    load_down.wait()
+
+    tall, short = CHUNK * 8, CHUNK * 4
+    row = lax.broadcasted_iota(jnp.int32, (short, tall), 0)
+    column = lax.broadcasted_iota(jnp.int32, (short, tall), 1)
+    at_low = lax.div(row, 4) * 8 + lax.rem(row, 4)
+    take_low = jnp.where(column == at_low, 1.0, 0.0).astype(bf16)
+    take_high = jnp.where(column == at_low + 4, 1.0, 0.0).astype(bf16)
+    row_t = lax.broadcasted_iota(jnp.int32, (tall, short), 0)
+    column_t = lax.broadcasted_iota(jnp.int32, (tall, short), 1)
+    at_low_t = lax.div(column_t, 4) * 8 + lax.rem(column_t, 4)
+    give_low = jnp.where(row_t == at_low_t, 1.0, 0.0).astype(bf16)
+    give_high = jnp.where(row_t == at_low_t + 4, 1.0, 0.0).astype(bf16)
+
+    def work(group, _):
+        a_rows = recv_a.at[pl.ds(group * tall, tall), :]
+        b_rows = recv_b.at[pl.ds(group * tall, tall), :]
+        pltpu.make_async_copy(a_rows, a_rows, in_a_sem.at[group]).wait()
+        pltpu.make_async_copy(b_rows, b_rows, in_b_sem.at[group]).wait()
+        rows[:tall, :] = a_rows[...]
+        rows[tall:, :half] = jnp.dot(
+            take_low, b_rows[...], preferred_element_type=f32
+        ).astype(bf16)
+        rows[tall:, half:] = jnp.dot(
+            take_high, b_rows[...], preferred_element_type=f32
+        ).astype(bf16)
+
+        def up(tile, _):
+            at = pl.multiple_of(tile * 256, 256)
+            first = jnp.dot(rows[...], gate_up[:, pl.ds(at, 256)], preferred_element_type=f32)
+            second = jnp.dot(
+                rows[...], gate_up[:, pl.ds(ff + at, 256)], preferred_element_type=f32
+            )
+            acts[:, pl.ds(at, 256)] = (jax.nn.silu(first) * second).astype(bf16)
+            return 0
+
+        lax.fori_loop(0, ff // 256, up, 0)
+
+        def lower(tile, _):
+            at = pl.multiple_of(tile * 512, 512)
+            result[:, pl.ds(at, 512)] = jnp.dot(
+                acts[...], down[:, pl.ds(at, 512)], preferred_element_type=f32
+            ).astype(bf16)
+            return 0
+
+        lax.fori_loop(0, width // 512, lower, 0)
+        back_a[pl.ds(group * tall, tall), :] = result[:tall, :]
+        mixed = jnp.dot(give_low, result[tall:, :half], preferred_element_type=f32)
+        mixed += jnp.dot(give_high, result[tall:, half:], preferred_element_type=f32)
+        back_b[pl.ds(group * tall, tall), :] = mixed.astype(bf16)
+
+        def give(k, _):
+            there = origin(here, k)
+            send(piece(back_a, k), piece(home_a, me), back_sem.at[0], home_sem.at[0], there).start()
+            send(piece(back_b, k), piece(home_b, me), back_sem.at[1], home_sem.at[1], there).start()
+            return 0
+
+        lax.fori_loop(jnp.where(group == 0, 1, group * CHUNK), (group + 1) * CHUNK, give, 0)
+        return 0
+
+    lax.fori_loop(0, 128 // CHUNK, work, 0)
+    own_c = pltpu.make_async_copy(piece(back_a, 0), piece(home_a, me), home_sem.at[0])
+    own_d = pltpu.make_async_copy(piece(back_b, 0), piece(home_b, me), home_sem.at[1])
+    own_c.start()
+    own_d.start()
+    pltpu.make_async_copy(home_a, home_a, home_sem.at[0]).wait()
+    pltpu.make_async_copy(home_b, home_b, home_sem.at[1]).wait()
+
+    out_ref[...] = jnp.zeros_like(out_ref)
+    over_rows = (((0,), (0,)), ((), ()))
+
+    def combine(part, _):
+        weight = gate_ref[pl.ds(part * 32, 32), :][:, None, :]
+
+        def add(wanted, values, columns):
+            exact = (choice(part, wanted) * weight).reshape(256, 128)
+            coarse = exact.astype(bf16)
+            fine = (exact - coarse.astype(f32)).astype(bf16)
+            out_ref[:, columns] += lax.dot_general(
+                coarse, values, over_rows, preferred_element_type=f32
+            ) + lax.dot_general(fine, values, over_rows, preferred_element_type=f32)
+
+        add(slot, home_a[pl.ds(part * 256, 256), :], slice(None))
+        values = home_b[pl.ds(part * 256, 256), :]
+        add(jnp.where(slot < 4, slot + 8, 99), values, slice(0, half))
+        add(jnp.where(slot >= 4, slot + 4, 99), values, slice(half, width))
+        return 0
+
+    lax.fori_loop(0, 4, combine, 0)
+    others = pl.ds(0, 127 * 8)
+    pltpu.make_async_copy(send_a.at[others], send_a.at[others], out_sem.at[0]).wait()
+    pltpu.make_async_copy(send_b.at[others], send_b.at[others], out_sem.at[1]).wait()
+    pltpu.make_async_copy(back_a.at[others], back_a.at[others], back_sem.at[0]).wait()
+    pltpu.make_async_copy(back_b.at[others], back_b.at[others], back_sem.at[1]).wait()
+
+
+def experts(moe_in, ids, gates, gate_up, down):
+    tokens, width = moe_in.shape
+    ff = down.shape[0]
+    groups = 128 // CHUNK
+    vmem = pl.BlockSpec(memory_space=pltpu.VMEM)
+    hbm = pl.BlockSpec(memory_space=pl.ANY)
+    a_shape = pltpu.VMEM((1024, width), jnp.bfloat16)
+    b_shape = pltpu.VMEM((1024, width // 2), jnp.bfloat16)
+    return pl.pallas_call(
+        moe_kernel,
+        out_shape=jax.ShapeDtypeStruct((tokens, width), jnp.float32),
+        in_specs=[vmem, vmem, vmem, hbm, hbm],
+        out_specs=vmem,
+        scratch_shapes=[
+            a_shape,
+            b_shape,
+            a_shape,
+            b_shape,
+            a_shape,
+            b_shape,
+            a_shape,
+            b_shape,
+            pltpu.VMEM((width, 2 * ff), jnp.bfloat16),
+            pltpu.VMEM((ff, width), jnp.bfloat16),
+            pltpu.VMEM((CHUNK * 12, width), jnp.bfloat16),
+            pltpu.VMEM((CHUNK * 12, ff), jnp.bfloat16),
+            pltpu.VMEM((CHUNK * 12, width), jnp.bfloat16),
+            pltpu.VMEM((128, 128), jnp.float32),
+            pltpu.VMEM((128, 128), jnp.float32),
+            pltpu.SemaphoreType.DMA((2,)),
+            pltpu.SemaphoreType.DMA((2,)),
+            pltpu.SemaphoreType.DMA((groups,)),
+            pltpu.SemaphoreType.DMA((groups,)),
+            pltpu.SemaphoreType.DMA((2,)),
+            pltpu.SemaphoreType.DMA((2,)),
+        ],
+        compiler_params=pltpu.CompilerParams(
+            collective_id=3, has_side_effects=True, vmem_limit_bytes=60 * 1024 * 1024
+        ),
+        cost_estimate=pl.CostEstimate(
+            flops=20_000_000_000, bytes_accessed=400_000_000, transcendentals=1_000_000
+        ),
+    )(moe_in, ids.T, gates.T, gate_up, down)
 
 
 def local(
@@ -97,8 +399,6 @@
     q_heads = query_width // head_dim
     head_split = q_heads // kv_heads
     scale = 1.0 / math.sqrt(head_dim)
-    row_count = lax.axis_size("dp")
-    col_count = lax.axis_size("expert")
     row = lax.axis_index("dp")
     col = lax.axis_index("expert")
     normed = root_mean_scale(hidden_in, attn_gain).astype(jnp.bfloat16)
@@ -182,28 +482,7 @@
     )
     mid = (hidden_in.astype(jnp.float32) + projected).astype(jnp.bfloat16)
     moe_in = root_mean_scale(mid, moe_gain).astype(jnp.bfloat16)
-    top_k = expert_ids.shape[1]
-    expert_count = row_count * col_count
-    capacity = max(2, tokens_here * top_k * 3 // (2 * expert_count))
-    flat = expert_ids.reshape(-1)
-    onehot = (flat[:, None] == jnp.arange(expert_count, dtype=jnp.int32)[None, :]).astype(jnp.int32)
-    slot = jnp.sum((jnp.cumsum(onehot, axis=0) - onehot) * onehot, axis=1)
-    place = flat * capacity + slot
-    sources = jnp.repeat(moe_in, top_k, axis=0)
-    outgoing = jnp.zeros((expert_count * capacity, width), jnp.bfloat16).at[place].set(sources)
-    gate_up = w_gate_up[0]
-    down = w_down[0]
-    received = lax.all_to_all(
-        outgoing.reshape(expert_count, capacity, width),
-        ("dp", "expert"),
-        split_axis=0,
-        concat_axis=0,
-        tiled=True,
-    )
-    results = expert_rows(received.reshape(-1, width), gate_up, down).reshape(received.shape)
-    returned = lax.all_to_all(results, ("dp", "expert"), split_axis=0, concat_axis=0, tiled=True)
-    picked = returned.reshape(expert_count * capacity, width)[place].astype(jnp.float32)
-    moe = jnp.sum(picked.reshape(tokens_here, top_k, width) * gate_weights[:, :, None], axis=1)
+    moe = experts(moe_in, expert_ids, gate_weights, w_gate_up[0], w_down[0])
     hidden_out = (mid.astype(jnp.float32) + moe).astype(jnp.bfloat16)
     return (hidden_out, suffix_cache)
 

time: 762 us -> 602 us (0.79); the launches traced: 754 us -> 602 us
  Pallas kernels: 0 us -> 156 us
  blocking collectives: 104 us -> 0 us
  waiting for transfers between devices: 382 us -> 300 us
  local copies, waits for them, and re-layouts: 102 us -> 23.1 us
  matrix products: 93.2 us -> 72.9 us
  other arithmetic: 51.6 us -> 35.6 us
    pallas_call x0 -> x1, Pallas kernels: none -> 156 us  [experts(): pl.pallas_call(moe_kernel, out_shape=jax.ShapeDtypeStruct((tokens, width)...]
    all_to_all x1 -> x0, blocking collectives: 104 us -> none  [local(): lax.all_to_all(outgoing.reshape(expert_count, capacity, width), ('dp', 'e...]
    all_to_all x1 -> x0, waiting for transfers between devices: 101 us -> none  [local(): lax.all_to_all(results, ('dp', 'expert'), split_axis=0, concat_axis=0, ti...]
    reshape x5 -> x1, local copies, waits for them, and re-layouts: 43.3 us -> 0.69 us  [the longest x1 10.7 us: local(): returned.reshape(expert_count * capacity, width)[place].astype(jnp.float32)]
    dot_general x2 -> x0, matrix products: 21.2 us -> none  [the longest x1 14.1 us: expert_rows(): both = jnp.dot(rows, gate_up, preferred_element_type=jnp.float32)]
    all_gather x1, waiting for transfers between devices: 21.2 us -> 35.8 us  [local(): piece = lax.all_gather(kv_pool, 'dp', axis=0, tiled=True)]
    gather x1 -> x0, local copies, waits for them, and re-layouts: 12.4 us -> none  [local(): returned.reshape(expert_count * capacity, width)[place].astype(jnp.float32)]
    scatter x1 -> x0, local copies, waits for them, and re-layouts: 10.9 us -> none  [local(): jnp.zeros((expert_count * capacity, width), jnp.bfloat16).at[place]]
  transfers between devices with their start and end apart: 6 -> 5, of which waited for: 6 -> 5; matrix products, arithmetic and copies ran while one was open for 18% -> 20% of each run, Pallas kernels for 0% -> 0%
where the time goes in v1:
time: 602 us
  waiting for transfers between devices  300 us (50%)
  Pallas kernels  156 us (26%)
  matrix products  72.9 us (12%)
  other arithmetic  35.6 us (6%)
  local copies, waits for them, and re-layouts  23.1 us (4%)
  between operations  14.1 us (2%)
    pallas_call x1, Pallas kernels, experts(): pl.pallas_call(moe_kernel, out_shape=jax.ShapeDtypeStruct((tokens, width)...  156 us
    all_gather x1, waiting for transfers between devices, local(): lax.all_gather(query_key_value_weight, 'expert', axis=0, tiled=True)  117 us
    all_gather x1, waiting for transfers between devices, local(): lax.all_gather(w_out, 'expert', axis=0, tiled=True)  72.7 us
    all_gather x1, waiting for transfers between devices, local(): piece_keys = lax.all_gather(key_rows, 'expert', axis=0, tiled=True)  42.9 us
    all_gather x1, waiting for transfers between devices, local(): piece = lax.all_gather(kv_pool, 'dp', axis=0, tiled=True)  35.8 us
    dot_general x2, matrix products, attend(): jnp.einsum('kgqs,skd->kgqd', weights.astype(jnp.bfloat16), value_rows, pr...  31.9 us
    dot_general x2, matrix products, attend(): jnp.einsum('qkgd,skd->kgqs', queries, key_rows, preferred_element_type=jn...  30.3 us
    all_gather x1, waiting for transfers between devices, local(): piece_values = lax.all_gather(value_rows, 'expert', axis=0, tiled=True)  30.3 us
  transfers between devices with their start and end apart: 5, of which 5 were waited for; matrix products, arithmetic and copies ran while one was open for 20% of the time, Pallas kernels for 0%

profile of v1, /device:TPU:1, one launch (start us, length us, event | category | flops | bytes accessed | tf_op | source)
XLA Modules:
  0.0 601.7 jit_solution(1438277594655784430)
XLA Ops:
  7.2 0.0 all-gather.6.cloned.1.call-start
  7.2 0.7 all-gather.6.cloned.1.call-update
  7.9 0.0 all-gather.12.cloned.1.call-start
  8.0 2.5 copy.64
  10.4 0.0 all-gather.12.cloned.1.call-update
  10.4 0.0 all-gather.8.cloned.1.call-start
  10.5 0.7 fusion.68
  11.2 0.2 reduce-window.4
  11.4 0.1 convert_reduce_fusion.1
  11.5 0.7 fusion.67
  12.2 0.1 select_reduce_fusion.1
  12.3 1.2 fusion.54
  13.5 0.3 multiply_cosine_fusion
  13.8 117.2 %all-gather.6.cloned.1.call-done = bf16[2048,2560]{1,0:T(8,128)(2,1)} async-done(((bf16[64,2560]{1,0:T(8,128)(2,1)}), bf16[2048,2560]{1,0:T(8,128)(2,1)}) %all-gather.6.cloned.1.call-update) | async-done | bytes 10485776 | tf_op jit(solution)/shard_map/all_gather | solution.py:408
  131.0 5.7 fusion.57
  136.8 0.0 copy-start.6
  136.8 0.1 reshape.279
  136.9 0.2 multiply_reduce_fusion.2
  137.1 0.1 copy.56
  137.2 0.0 copy-done.5
  137.2 0.1 fusion.61
  137.3 0.1 multiply_subtract_fusion
  137.4 0.7 maximum_convert_fusion
  138.1 0.0 all-gather.8.cloned.1.call-update
  138.2 0.0 all-gather.10.cloned.1.call-start
  138.2 0.7 copy.73
  138.9 0.0 all-gather.10.cloned.1.call-update
  139.0 0.2 all-gather.14.cloned.1.call-start
  139.2 0.4 all-gather.14.cloned.1.call-update
  139.6 0.1 select_reduce_fusion
  139.7 0.1 convert_reduce_fusion
  139.8 0.1 broadcast_bitcast_fusion
  139.9 0.4 broadcast_compare_fusion
  140.3 1.9 fusion.18
  142.1 35.8 %all-gather.12.cloned.1.call-done = bf16[32,2,128,2,128]{4,2,3,1,0:T(8,128)(2,1)} async-done(((bf16[8,2,128,2,128]{4,2,3,1,0:T(8,128)(2,1)}), bf16[32,2,128,2,128]{4,2,3,1,0:T(8,128)(2,1)}) %all-gather.12.cloned.1.call-update) | async-done | bytes 4194320 | tf_op jit(solution)/shard_map/all_gather | solution.py:456
  178.0 4.1 fusion.77
  182.1 1.6 copy.65
  183.7 3.5 copy.66
  187.1 2.4 reshape.285
  189.5 1.3 slice_bitcast_fusion
  190.8 0.2 copy.76
  191.0 0.3 multiply_reduce_fusion.1
  191.4 0.1 copy.58
  191.4 0.1 copy.59
  191.6 0.3 multiply_multiply_fusion
  191.9 0.5 subtract_convert_fusion
  192.5 0.1 copy.60
  192.6 0.1 copy.61
  192.7 0.1 copy_bitcast_fusion
  192.8 0.7 pad_maximum_fusion.1
  193.5 15.5 %bitcast_reduce_fusion = (f32[2,8,128]{2,1,0:T(8,128)S(1)}, f32[2,128,8,4096]{3,1,2,0:T(8,128)}) fusion(pred[128,4096]{1,0:T(8,128)(4,1)S(1)} %broadcast_compare_fusion, bf16[4096,2,128,1]{2,0,3,1:T(8,128)(2,1)} %bitcast.147, bf16[128,2,8,64]{3,0,2,1:T(8,128)(2,1)S(1)} %bitcast.150, bf16[128,2,8,64]{3,0,2,1:T(8,128)(2,1)S(1)} %bitcast.148), kind=kOutput, calls=%fused_computation.1 | convolution fusion | flops 2173696000 | bytes 36708352 | tf_op jit(solution)/shard_map/qkgd,skd->kgqs/dot_general | solution.py:53
  209.0 42.9 %all-gather.8.cloned.1.call-done = bf16[4096,2,128]{2,0,1:T(8,128)(2,1)} async-done(((bf16[128,2,128]{2,0,1:T(8,128)(2,1)}), bf16[4096,2,128]{2,0,1:T(8,128)(2,1)}) %all-gather.8.cloned.1.call-update) | async-done | bytes 2097168 | tf_op jit(solution)/shard_map/all_gather | solution.py:448
  251.9 14.8 %fusion.3 = (f32[2,8,128]{2,1,0:T(8,128)S(1)}, f32[2,4096,128,8]{2,1,3,0:T(8,128)}) fusion(pred[128,4096]{0,1:T(8,128)(4,1)S(1)} %fusion.18, bf16[128,2,8,64]{3,0,2,1:T(8,128)(2,1)S(1)} %bitcast.151, bf16[128,2,8,64]{3,0,2,1:T(8,128)(2,1)S(1)} %bitcast.149, bf16[4096,2,128]{2,0,1:T(8,128)(2,1)} %all-gather.8.cloned.1.call-done), kind=kOutput, calls=%fused_computation.8 | convolution fusion | flops 2173696000 | bytes 36708352 | tf_op jit(solution)/shard_map/qkgd,skd->kgqs/dot_general | solution.py:53
  266.7 14.8 %fusion.1 = f32[2,8,128]{2,1,0:T(8,128)S(1)} fusion(f32[2,4096,128,8]{2,1,3,0:T(8,128)} %get-tuple-element.22, f32[2,8,128]{2,1,0:T(8,128)S(1)} %get-tuple-element.16, pred[128,4096]{0,1:T(8,128)(4,1)S(1)} %fusion.18), kind=kLoop, calls=%fused_computation.6 | loop fusion | flops 33552384 | bytes 34095104 | tf_op jit(solution)/shard_map/reduce_sum | solution.py:59
  281.5 5.5 copy-done
  287.0 9.5 %fusion.4 = f32[2,8,128]{2,1,0:T(8,128)S(1)} fusion(f32[2,128,8,4096]{3,1,2,0:T(8,128)S(1)} %copy-done, f32[2,8,128]{2,1,0:T(8,128)S(1)} %get-tuple-element.15, pred[128,4096]{1,0:T(8,128)(4,1)S(1)} %broadcast_compare_fusion), kind=kLoop, calls=%fused_computation.9 | loop fusion | flops 33552384 | bytes 34095104 | tf_op jit(solution)/shard_map/reduce_sum | solution.py:59
  296.5 30.3 %all-gather.10.cloned.1.call-done = bf16[4096,2,128]{0,2,1:T(8,128)(2,1)} async-done(((bf16[128,2,128]{0,2,1:T(8,128)(2,1)}), bf16[4096,2,128]{0,2,1:T(8,128)(2,1)}) %all-gather.10.cloned.1.call-update) | async-done | bytes 2097168 | tf_op jit(solution)/shard_map/all_gather | solution.py:449
  326.8 16.1 %fusion.39 = f32[128,2,8,128]{0,3,2,1:T(8,128)} fusion(f32[2,4096,128,8]{2,1,3,0:T(8,128)} %get-tuple-element.22, f32[2,8,128]{2,1,0:T(8,128)S(1)} %get-tuple-element.16, pred[128,4096]{0,1:T(8,128)(4,1)S(1)} %fusion.18, bf16[4096,2,128]{0,2,1:T(8,128)(2,1)} %all-gather.10.cloned.1.call-done, f32[128,2,8]{0,2,1:T(8,128)S(1)} %get-tuple-element.5, ...), kind=kOutput, calls=%fused_computation.30 | convolution fusion | flops 2181562368 | bytes 37249024 | tf_op jit(solution)/shard_map/kgqs,skd->kgqd/dot_general | solution.py:60
  342.9 15.8 %fusion.49 = bf16[128,2,8,128]{0,3,2,1:T(8,128)(2,1)} fusion(f32[128,2,8,128]{0,3,2,1:T(8,128)} %fusion.39, bf16[4096,2,128,1]{0,2,1,3:T(8,128)(2,1)S(1)} %copy-done.3, f32[2,128,8,4096]{3,1,2,0:T(8,128)} %get-tuple-element.20, f32[2,8,128]{2,1,0:T(8,128)S(1)} %get-tuple-element.15, pred[128,4096]{1,0:T(8,128)(4,1)S(1)} %broadcast_compare_fusion, ...), kind=kOutput, calls=%fused_computation.32 | convolution fusion | flops 2181824512 | bytes 37765120 | tf_op jit(solution)/shard_map/kgqs,skd->kgqd/dot_general | solution.py:60
  358.7 72.7 %all-gather.14.cloned.1.call-done = bf16[2048,2048]{1,0:T(8,128)(2,1)} async-done(((bf16[64,2048]{1,0:T(8,128)(2,1)}), bf16[2048,2048]{1,0:T(8,128)(2,1)}) %all-gather.14.cloned.1.call-update) | async-done | bytes 8388624 | tf_op jit(solution)/shard_map/all_gather | solution.py:480
  431.4 4.9 multiply_reduce_fusion
  436.3 0.9 multiply_convert_fusion.x_ref
  437.3 155.8 %shard_map.158 = f32[128,2048]{1,0:T(8,128)} custom-call(bf16[128,2048]{1,0:T(8,128)(2,1)} %multiply_convert_fusion.x_ref, s32[8,128]{1,0:T(8,128)} %bitcast.158, f32[8,128]{1,0:T(8,128)} %bitcast.159, bf16[2048,1536]{1,0:T(8,128)(2,1)} %bitcast.156, bf16[768,2048]{1,0:T(8,128)(2,1)} %bitcast.157), custom_call_target="tpu_custom_call" | custom-call | flops 20000000000 | bytes 400000000 | tf_op jit(solution)/shard_map/pallas_call | solution.py:339
  593.1 2.1 add_convert_fusion
  (25 shorter events, 0.1 us)
Async XLA Ops:
  7.2 130.0 %copy-start.5 = (f32[128]{0:T(128)S(1)}, f32[128]{0:T(128)}, u32[]{:S(2)}) copy-start(f32[128]{0:T(128)} %param.19) | copy-start | bytes 1540
  7.2 132.4 %copy-start.7 = (s32[32]{0:T(128)S(1)}, s32[32]{0:T(128)}, u32[]{:S(2)}) copy-start(s32[32]{0:T(128)} %param.25) | copy-start | bytes 388
  7.2 123.8 %all-gather.6.cloned.1.call-start = ((), (), s32[]{:S(2)}) async-start(), calls=%async_computation | async-start | bytes 10813440 | tf_op jit(solution)/shard_map/all_gather | solution.py:408
  7.9 170.1 %all-gather.12.cloned.1.call-start = ((), (), s32[]{:S(2)}) async-start(), calls=%async_computation.3 | async-start | bytes 5242880 | tf_op jit(solution)/shard_map/all_gather | solution.py:456
  10.4 241.4 %all-gather.8.cloned.1.call-start = ((), (), s32[]{:S(2)}) async-start(), calls=%async_computation.1 | async-start | bytes 2162688 | tf_op jit(solution)/shard_map/all_gather | solution.py:448
  136.8 3.1 copy-start.2
  136.8 54.8 %copy-start.6 = (f32[128]{0:T(128)S(1)}, f32[128]{0:T(128)}, u32[]{:S(2)}) copy-start(f32[128]{0:T(128)} %param.18) | copy-start | bytes 1540
  138.2 188.6 %all-gather.10.cloned.1.call-start = ((), (), s32[]{:S(2)}) async-start(), calls=%async_computation.2 | async-start | bytes 2162688 | tf_op jit(solution)/shard_map/all_gather | solution.py:449
  139.0 292.4 %all-gather.14.cloned.1.call-start = ((), (), s32[]{:S(2)}) async-start(), calls=%async_computation.4 | async-start | bytes 8650752 | tf_op jit(solution)/shard_map/all_gather | solution.py:480
  266.7 20.3 %copy-start = (f32[2,128,8,4096]{3,1,2,0:T(8,128)S(1)}, f32[2,128,8,4096]{3,1,2,0:T(8,128)}, u32[]{:S(2)}) copy-start(f32[2,128,8,4096]{3,1,2,0:T(8,128)} %get-tuple-element.20) | copy-start | bytes 100663296
  326.8 16.1 %copy-start.3 = (bf16[4096,2,128,1]{0,2,1,3:T(8,128)(2,1)S(1)}, bf16[4096,2,128,1]{0,2,1,3:T(8,128)(2,1)}, u32[]{:S(2)}) copy-start(bf16[4096,2,128,1]{0,2,1,3:T(8,128)(2,1)} %reshape.285) | copy-start | bytes 6291460
  342.9 88.5 %copy-start.1 = (bf16[128,2048]{1,0:T(8,128)(2,1)S(1)}, bf16[128,2048]{1,0:T(8,128)(2,1)}, u32[]{:S(2)}) copy-start(bf16[128,2048]{1,0:T(8,128)(2,1)} %param.15) | copy-start | bytes 1572868
  358.7 77.6 %copy-start.4 = (f32[2048]{0:T(1024)S(1)}, f32[2048]{0:T(1024)}, u32[]{:S(2)}) copy-start(f32[2048]{0:T(1024)} %param.21) | copy-start | bytes 24580
Sparse Core Ops, SparseCore 0:
  11.1 119.8 all-gather.5
  132.7 45.2 all-gather.11
  181.8 70.0 all-gather.7
  254.5 72.2 all-gather.9
  329.7 101.6 all-gather.13

commit v2 on v1

--- a/solution.py
+++ b/solution.py
@@ -8,7 +8,6 @@
 from jax.sharding import PartitionSpec as P
 
 PREFIX_TOKENS = 2048
-PAGE_TOKENS = 128
 
 
 eps = 1e-06
@@ -23,47 +22,6 @@
         * lax.rsqrt(jnp.mean(value_rows * value_rows, axis=-1, keepdims=True) + eps)
         * gain
     )
-
-
-def rotary_apply(value_rows, token_positions):
-    half = value_rows.shape[-1] // 2
-    freqs = theta ** (-jnp.arange(half, dtype=jnp.float32) / half)
-    angles = token_positions.astype(jnp.float32)[:, None] * freqs[None, :]
-    cosine = jnp.cos(angles)[:, None, :]
-    sine = jnp.sin(angles)[:, None, :]
-    first = value_rows[..., :half]
-    second_split = value_rows[..., half:]
-    return jnp.concatenate(
-        [first * cosine - second_split * sine, second_split * cosine + first * sine], axis=-1
-    )
-
-
-def layout(lengths_row, index):
-    ends = jnp.cumsum(lengths_row)
-    starts = ends - lengths_row
-    request = jnp.sum((index[:, None] >= ends[None, :]).astype(jnp.int32), axis=1)
-    chosen = request[:, None] == jnp.arange(lengths_row.shape[0], dtype=jnp.int32)[None, :]
-    offset = index - jnp.sum(jnp.where(chosen, starts[None, :], 0), axis=1)
-    return (request, offset, chosen)
-
-
-def attend(carry, queries, key_rows, value_rows, mask, scale):
-    high, total, acc = carry
-    scores = (
-        jnp.einsum("qkgd,skd->kgqs", queries, key_rows, preferred_element_type=jnp.float32) * scale
-    )
-    scores = jnp.where(mask[None, None], scores, -jnp.inf)
-    new_high = jnp.maximum(high, jnp.max(scores, axis=-1))
-    weights = jnp.exp(scores - new_high[..., None])
-    scale_factor = jnp.exp(high - new_high)
-    total = total * scale_factor + jnp.sum(weights, axis=-1)
-    acc = acc * scale_factor[..., None] + jnp.einsum(
-        "kgqs,skd->kgqd",
-        weights.astype(jnp.bfloat16),
-        value_rows,
-        preferred_element_type=jnp.float32,
-    )
-    return (new_high, total, acc)
 
 
 MESH_ID = pl.DeviceIdType.MESH
@@ -373,6 +331,401 @@
     )(moe_in, ids.T, gates.T, gate_up, down)
 
 
+def arrived(ref, sem):
+    pltpu.make_async_copy(ref, ref, sem).wait()
+
+
+class Gather:
+    def __init__(self, buf, here, cross, columns, sems):
+        self.buf, self.here, self.cross, self.columns = buf, here, cross, columns
+        self.send_sem, self.recv_sem, self.cross_sem = sems
+
+    def cut(self, r):
+        start, size = self.columns[r]
+        return pl.ds(pl.multiple_of(start, 128), size)
+
+    def whole(self, h):
+        x, y, z, c = self.here
+        start, size = self.columns[0]
+        return self.buf.at[y, h, z, :, pl.ds(pl.multiple_of(start, 128), size + self.columns[1][1])]
+
+    def near(self, r):
+        x, y, z, c = self.here
+        cut = self.cut(r)
+        if r == 0:
+            return lambda p, h: self.buf.at[y, h, p, :, cut]
+        return lambda p, h: self.buf.at[p, h, z, :, cut]
+
+    def far(self, r):
+        cut = self.cut(r)
+        if r == 0:
+            return lambda p, h: self.buf.at[p, h, :, :, cut]
+        return lambda p, h: self.buf.at[:, h, p, :, cut]
+
+    def ring(self, r, phase):
+        x, y, z, c = self.here
+        if (r + phase) % 2 == 0:
+            return z, (x, y, lax.rem(z + 1, 4), c), (x, y, lax.rem(z + 3, 4), c)
+        return y, (x, lax.rem(y + 1, 4), z, c), (x, lax.rem(y + 3, 4), z, c)
+
+    def start(self):
+        own = lax.div(self.here[0], 2)
+        send(
+            self.whole(own), self.whole(own), self.cross_sem.at[0], self.cross_sem.at[1], self.cross
+        ).start()
+        self.push(0, own)
+
+    def push(self, phase, h):
+        for r in range(2):
+            pick = (self.near if phase == 0 else self.far)(r)
+            pos, right, left = self.ring(r, phase)
+            piece = pick(pos, h)
+            for d, there in enumerate((right, left)):
+                send(
+                    piece,
+                    piece,
+                    self.send_sem.at[r, phase, d, h],
+                    self.recv_sem.at[r, phase, d, h],
+                    there,
+                ).start()
+
+    def first(self):
+        own = lax.div(self.here[0], 2)
+        arrived(self.whole(1 - own), self.cross_sem.at[1])
+        self.push(0, 1 - own)
+        self.forward(0)
+        self.rest(0, None)
+
+    def forward(self, phase):
+        for d in range(2):
+            for r in range(2):
+                pick = (self.near if phase == 0 else self.far)(r)
+                pos, right, left = self.ring(r, phase)
+                arrived(pick(pos, d), self.recv_sem.at[r, phase, d, d])
+                piece = pick(lax.rem(pos + (3 if d == 0 else 1), 4), d)
+                send(
+                    piece,
+                    piece,
+                    self.send_sem.at[r, phase, 2, d],
+                    self.recv_sem.at[r, phase, 2, d],
+                    right if d == 0 else left,
+                ).start()
+
+    def rest(self, phase, seen):
+        for d, h in ((0, 1), (1, 0), (2, 0), (2, 1)):
+            for r in range(2):
+                pick = (self.near if phase == 0 else self.far)(r)
+                pos, _, _ = self.ring(r, phase)
+                arrived(pick(pos, h), self.recv_sem.at[r, phase, d, h])
+                if seen is not None:
+                    seen(r, d, h, pick(lax.rem(pos + (3, 1, 2)[d], 4), h))
+
+    def second(self, seen=None):
+        self.push(1, 0)
+        self.push(1, 1)
+        self.forward(1)
+        if seen is not None:
+            for d in range(2):
+                for r in range(2):
+                    pos, _, _ = self.ring(r, 1)
+                    seen(r, d, d, self.far(r)(lax.rem(pos + (3, 1)[d], 4), d))
+        self.rest(1, seen)
+
+    def drain(self):
+        arrived(self.whole(0), self.cross_sem.at[0])
+        for r in range(2):
+            for phase in range(2):
+                pick = (self.near if phase == 0 else self.far)(r)
+                for d in range(3):
+                    for h in range(2):
+                        arrived(pick(0, h), self.send_sem.at[r, phase, d, h])
+
+
+def front_kernel(
+    hidden_ref,
+    gain_ref,
+    shard_ref,
+    q_gain_ref,
+    k_gain_ref,
+    cos_ref,
+    sin_ref,
+    q_ref,
+    kv_ref,
+    cache_ref,
+    weight,
+    qkv,
+    normed_ref,
+    w_send,
+    w_recv,
+    w_cross,
+    k_send,
+    k_recv,
+    k_cross,
+    swap_send,
+    swap_recv,
+    local_sem,
+):
+    f32, bf16 = jnp.float32, jnp.bfloat16
+    here = place()
+    x, y, z, c = here
+    own = lax.div(x, 2)
+    columns = weight.shape[-1]
+    side = columns // 2
+    turn = side // 2
+    partner = (x, y, z, 1 - c)
+    even = 1 - lax.rem(x, 2)
+    across = (lax.rem(x + 1 + 2 * even, 4), y, z, c)
+    opposite = (lax.rem(x + 2, 4), y, z, c)
+    barrier = pltpu.get_barrier_semaphore()
+    peers = (
+        partner,
+        across,
+        opposite,
+        (x, lax.rem(y + 1, 4), z, c),
+        (x, lax.rem(y + 3, 4), z, c),
+        (x, y, lax.rem(z + 1, 4), c),
+        (x, y, lax.rem(z + 3, 4), c),
+    )
+    for peer in peers:
+        pl.semaphore_signal(barrier, inc=1, device_id=device(*peer), device_id_type=MESH_ID)
+    mine = pl.ds(pl.multiple_of(c * side, 128), side)
+    seed = pltpu.make_async_copy(
+        shard_ref.at[:, mine], weight.at[y, own, z, :, mine], local_sem
+    )
+    seed.start()
+    seed.wait()
+    pl.semaphore_wait(barrier, len(peers))
+
+    gather = Gather(
+        weight,
+        here,
+        across,
+        ((c * side, turn), (c * side + turn, side - turn)),
+        (w_send, w_recv, w_cross),
+    )
+    gather.start()
+
+    value = hidden_ref[...].astype(f32)
+    mean = jnp.mean(value * value, axis=-1, keepdims=True)
+    normed_ref[...] = (value * lax.rsqrt(mean + eps) * gain_ref[...]).astype(bf16)
+
+    gather.first()
+    swaps = []
+
+    def swap(r, slot, piece):
+        copy = send(piece, piece, swap_send.at[r, slot], swap_recv.at[r, slot], partner)
+        copy.start()
+        swaps.append(copy)
+
+    gather.push(1, 0)
+    gather.push(1, 1)
+    for r in range(2):
+        pos, _, _ = gather.ring(r, 1)
+        cut = gather.cut(r)
+        whole = weight.at[pos, :, :, :, cut] if r == 0 else weight.at[:, :, pos, :, cut]
+        swap(r, 6, whole)
+    gather.forward(1)
+    for d in range(2):
+        for r in range(2):
+            pos, _, _ = gather.ring(r, 1)
+            swap(r, d * 2 + d, gather.far(r)(lax.rem(pos + (3, 1)[d], 4), d))
+    gather.rest(1, lambda r, d, h, piece: swap(r, d * 2 + h, piece))
+    for copy in swaps:
+        copy.wait_recv()
+
+    span = 2 * 4 * weight.shape[3]
+
+    def project(tile, _):
+        at = pl.multiple_of(tile * 512, 512)
+        total = jnp.zeros((normed_ref.shape[0], 512), f32)
+        for plane in range(4):
+            block = weight[plane, :, :, :, pl.ds(at, 512)].reshape(span, 512)
+            total += jnp.dot(
+                normed_ref[:, plane * span : (plane + 1) * span],
+                block,
+                preferred_element_type=f32,
+            )
+        qkv[:, pl.ds(at, 512)] = total
+        return 0
+
+    lax.fori_loop(0, columns // 512, project, 0)
+
+    cosine = cos_ref[...]
+    sine = sin_ref[...]
+    heads = columns // 128
+
+    def turned(head, gain):
+        rows = qkv[:, pl.ds(pl.multiple_of(head * 128, 128), 128)]
+        mean = jnp.mean(rows * rows, axis=-1, keepdims=True)
+        rows = rows * lax.rsqrt(mean + eps) * gain
+        return (rows * cosine + pltpu.roll(rows, 64, 1) * sine).astype(bf16)
+
+    for h in range(2):
+        cache_ref[:, h * 128 : (h + 1) * 128] = turned(heads - 4 + h, k_gain_ref[...])
+    cache_ref[:, 256:512] = qkv[:, columns - 256 :].astype(bf16)
+    seed = pltpu.make_async_copy(cache_ref, kv_ref.at[y, own, z], local_sem)
+    seed.start()
+    seed.wait()
+    spread = Gather(kv_ref, here, opposite, ((0, 256), (256, 256)), (k_send, k_recv, k_cross))
+    spread.start()
+
+    def query(head, _):
+        at = pl.multiple_of(lax.rem(head, 8) * 128, 128)
+        q_ref[lax.div(head, 8), pl.ds(at, 128), :] = turned(head, q_gain_ref[...])
+        return 0
+
+    lax.fori_loop(0, heads - 4, query, 0)
+    spread.first()
+    spread.second()
+    gather.drain()
+    spread.drain()
+    for copy in swaps:
+        copy.wait_send()
+
+
+def front(hidden, gain, shard, q_gain, k_gain, cosine, sine):
+    tokens, width = hidden.shape
+    rows, columns = shard.shape
+    vmem = pl.BlockSpec(memory_space=pltpu.VMEM)
+    ring = pltpu.SemaphoreType.DMA((2, 2, 3, 2))
+    two = pltpu.SemaphoreType.DMA((2,))
+    swap = pltpu.SemaphoreType.DMA((2, 7))
+    return pl.pallas_call(
+        front_kernel,
+        out_shape=(
+            jax.ShapeDtypeStruct((2, 8 * tokens, 128), jnp.bfloat16),
+            jax.ShapeDtypeStruct((4, 2, 4, tokens, 512), jnp.bfloat16),
+            jax.ShapeDtypeStruct((tokens, 512), jnp.bfloat16),
+        ),
+        in_specs=[vmem] * 7,
+        out_specs=(vmem, vmem, vmem),
+        scratch_shapes=[
+            pltpu.VMEM((4, 2, 4, rows, columns), jnp.bfloat16),
+            pltpu.VMEM((tokens, columns), jnp.float32),
+            pltpu.VMEM((tokens, width), jnp.bfloat16),
+            ring,
+            ring,
+            two,
+            ring,
+            ring,
+            two,
+            swap,
+            swap,
+            pltpu.SemaphoreType.DMA,
+        ],
+        compiler_params=pltpu.CompilerParams(
+            collective_id=1, has_side_effects=True, vmem_limit_bytes=56 * 1024 * 1024
+        ),
+        cost_estimate=pl.CostEstimate(
+            flops=1_400_000_000, bytes_accessed=200_000_000, transcendentals=1_000_000
+        ),
+    )(hidden, gain, shard, q_gain, k_gain, cosine, sine)
+
+
+def attention_kernel(
+    facts, table, q_ref, kv_ref, pool_ref, start_ref, index_ref, group_ref, out_ref, high, total, acc
+):
+    f32, bf16 = jnp.float32, jnp.bfloat16
+    factor = math.log2(math.e) / math.sqrt(128)
+    high[...] = jnp.full_like(high, floor_value)
+    total[...] = jnp.zeros_like(total)
+    acc[...] = jnp.zeros_like(acc)
+
+    def step(h, keys, values, seen):
+        scores = lax.dot_general(
+            keys, q_ref[h], (((1,), (1,)), ((), ())), preferred_element_type=f32
+        )
+        if seen is not None:
+            scores = jnp.where(jnp.concatenate([seen] * 8, axis=1), scores, -jnp.inf)
+        old = high[h]
+        new = jnp.maximum(old, jnp.max(scores, axis=0, keepdims=True))
+        weights = jnp.exp2((scores - new) * factor)
+        shrink = jnp.exp2((old - new) * factor)
+        high[h] = new
+        total[h] = total[h] * shrink + jnp.sum(weights, axis=0, keepdims=True)
+        acc[h] = acc[h] * shrink + lax.dot_general(
+            values, weights.astype(bf16), (((0,), (0,)), ((), ())), preferred_element_type=f32
+        )
+
+    span = 4
+    for group in range(2):
+
+        def pages(seen, group=group):
+            def body(j, _):
+                picked = [table[group * 16 + j * span + i] for i in range(span)]
+                for h in range(2):
+                    keys = jnp.concatenate([pool_ref[p, 0, h] for p in picked], axis=0)
+                    values = jnp.concatenate([pool_ref[p, 1, h] for p in picked], axis=0)
+                    step(h, keys, values, seen)
+                return 0
+
+            lax.fori_loop(0, 16 // span, body, 0)
+
+        @pl.when(facts[group] == 2)
+        def _():
+            pages(None)
+
+        @pl.when(facts[group] == 1)
+        def _():
+            pages(jnp.broadcast_to(group_ref[...] == group, (span * 128, 128)))
+
+    size = 256
+
+    def suffix(tile, masked):
+        at = pl.multiple_of(tile * size, size)
+        seen = None
+        if masked:
+            place_of = at + lax.broadcasted_iota(jnp.int32, (size, 128), 0)
+            seen = (place_of >= start_ref[...]) & (place_of <= index_ref[...])
+        for h in range(2):
+            keys = kv_ref[pl.ds(at, size), h * 128 : (h + 1) * 128]
+            values = kv_ref[pl.ds(at, size), 256 + h * 128 : 256 + (h + 1) * 128]
+            step(h, keys, values, seen)
+
+    def tiles(tile, _):
+        clear = (tile * size >= facts[3]) & (tile * size + size <= facts[4] + 1)
+
+        @pl.when(clear)
+        def _():
+            suffix(tile, False)
+
+        @pl.when(jnp.logical_not(clear))
+        def _():
+            suffix(tile, True)
+
+        return 0
+
+    lax.fori_loop(lax.div(facts[2], size), lax.div(facts[5], size) + 1, tiles, 0)
+    for h in range(2):
+        done = acc[h] / total[h]
+        for g in range(8):
+            head = h * 8 + g
+            out_ref[:, head * 128 : (head + 1) * 128] = (
+                done[:, g * 128 : (g + 1) * 128].T.astype(bf16)
+            )
+
+
+def attention(facts, table, q, kv, pool, start, index, group):
+    vmem = pl.BlockSpec(memory_space=pltpu.VMEM)
+    smem = pl.BlockSpec(memory_space=pltpu.SMEM)
+    tokens = start.shape[1]
+    return pl.pallas_call(
+        attention_kernel,
+        out_shape=jax.ShapeDtypeStruct((tokens, 16 * 128), jnp.bfloat16),
+        in_specs=[smem, smem] + [vmem] * 6,
+        out_specs=vmem,
+        scratch_shapes=[
+            pltpu.VMEM((2, 1, 8 * tokens), jnp.float32),
+            pltpu.VMEM((2, 1, 8 * tokens), jnp.float32),
+            pltpu.VMEM((2, 128, 8 * tokens), jnp.float32),
+        ],
+        compiler_params=pltpu.CompilerParams(vmem_limit_bytes=56 * 1024 * 1024),
+        cost_estimate=pl.CostEstimate(
+            flops=5_000_000_000, bytes_accessed=10_000_000, transcendentals=10_000_000
+        ),
+    )(facts, table, q, kv, pool, start, index, group)
+
+
 def local(
     hidden_in,
     attn_gain,
@@ -391,95 +744,58 @@
     gate_weights,
 ):
     tokens_here, width = hidden_in.shape
-    page_rows = kv_pool.shape[2]
-    kv_heads = kv_pool.shape[3]
-    head_dim = kv_pool.shape[4]
-    key_value_width = kv_heads * head_dim
-    query_width = query_key_value_weight.shape[1] - 2 * key_value_width
-    q_heads = query_width // head_dim
-    head_split = q_heads // kv_heads
-    scale = 1.0 / math.sqrt(head_dim)
     row = lax.axis_index("dp")
     col = lax.axis_index("expert")
-    normed = root_mean_scale(hidden_in, attn_gain).astype(jnp.bfloat16)
-    part = normed
-    qkv = jnp.dot(
-        part,
-        lax.all_gather(query_key_value_weight, "expert", axis=0, tiled=True),
-        preferred_element_type=jnp.float32,
-    )
+    pool = lax.all_gather(kv_pool.transpose(0, 1, 3, 2, 4), "dp", axis=0, tiled=True)
+    w_out_all = lax.all_gather(w_out, "expert", axis=0, tiled=True)
     index = col * tokens_here + jnp.arange(tokens_here, dtype=jnp.int32)
     lengths_row = lax.dynamic_index_in_dim(suffix_lengths, row, 0, keepdims=False)
     groups_row = lax.dynamic_index_in_dim(request_group, row, 0, keepdims=False)
-    request, offset, chosen = layout(lengths_row, index)
-    qgroup = jnp.sum(jnp.where(chosen, groups_row[None, :], 0), axis=1)
-    token_positions = PREFIX_TOKENS + offset
-    queries = rotary_apply(
-        root_mean_scale(qkv[:, :query_width].reshape(tokens_here, q_heads, head_dim), q_gain),
-        token_positions,
-    ).astype(jnp.bfloat16)
-    key_rows = rotary_apply(
-        root_mean_scale(
-            qkv[:, query_width : query_width + key_value_width].reshape(
-                tokens_here, kv_heads, head_dim
-            ),
-            key_norm_gain,
-        ),
-        token_positions,
-    ).astype(jnp.bfloat16)
-    value_rows = (
-        qkv[:, query_width + key_value_width :]
-        .reshape(tokens_here, kv_heads, head_dim)
-        .astype(jnp.bfloat16)
-    )
-    suffix_cache = jnp.concatenate(
+    ends = [lengths_row[0]]
+    for r in range(1, 4):
+        ends.append(ends[-1] + lengths_row[r])
+    start = jnp.zeros_like(index)
+    group = jnp.full_like(index, 0) + groups_row[0]
+    for r in range(3):
+        later = index >= ends[r]
+        start = jnp.where(later, ends[r], start)
+        group = jnp.where(later, groups_row[r + 1], group)
+    offset = index - start
+    half = 64
+    freqs = theta ** (-jnp.arange(half, dtype=jnp.float32) / half)
+    angles = (PREFIX_TOKENS + offset).astype(jnp.float32)[:, None] * freqs[None, :]
+    cosine, sine = jnp.cos(angles), jnp.sin(angles)
+    q, kv, suffix_cache = front(
+        hidden_in,
+        attn_gain[None],
+        query_key_value_weight,
+        q_gain[None],
+        key_norm_gain[None],
+        jnp.concatenate([cosine, cosine], axis=1),
+        jnp.concatenate([-sine, sine], axis=1),
+    )
+    ones = jnp.sum(group)
+    facts = jnp.stack(
         [
-            key_rows.reshape(tokens_here, key_value_width),
-            value_rows.reshape(tokens_here, key_value_width),
-        ],
-        axis=1,
-    )
-    grouped = queries.reshape(tokens_here, kv_heads, head_split, head_dim)
-    carry = (
-        jnp.full((kv_heads, head_split, tokens_here), floor_value, jnp.float32),
-        jnp.zeros((kv_heads, head_split, tokens_here), jnp.float32),
-        jnp.zeros((kv_heads, head_split, tokens_here, head_dim), jnp.float32),
-    )
-    piece_keys = lax.all_gather(key_rows, "expert", axis=0, tiled=True)
-    piece_values = lax.all_gather(value_rows, "expert", axis=0, tiled=True)
-    key_index = jnp.arange(piece_keys.shape[0], dtype=jnp.int32)
-    key_request, _, _ = layout(lengths_row, key_index)
-    mask = (key_request[None, :] == request[:, None]) & (key_index[None, :] <= index[:, None])
-    carry = attend(carry, grouped, piece_keys, piece_values, mask, scale)
-    per_group = PREFIX_TOKENS // PAGE_TOKENS
-    slot_ids = jnp.arange(page_table.shape[0], dtype=jnp.int32)
-    piece = lax.all_gather(kv_pool, "dp", axis=0, tiled=True)
-    count = piece.shape[0]
-    hit = page_table[None, :] == jnp.arange(count, dtype=jnp.int32)[:, None]
-    key_group = jnp.repeat(
-        jnp.sum(jnp.where(hit, slot_ids[None, :] // per_group, 0), axis=1), page_rows
-    )
-    mask = key_group[None, :] == qgroup[:, None]
-    carry = attend(
-        carry,
-        grouped,
-        piece[:, 0].reshape(count * page_rows, kv_heads, head_dim),
-        piece[:, 1].reshape(count * page_rows, kv_heads, head_dim),
-        mask,
-        scale,
-    )
-    mixed = (
-        (carry[2] / carry[1][..., None])
-        .transpose(2, 0, 1, 3)
-        .reshape(tokens_here, query_width)
-        .astype(jnp.bfloat16)
-    )
-    part = mixed
-    projected = jnp.dot(
-        part,
-        lax.all_gather(w_out, "expert", axis=0, tiled=True),
-        preferred_element_type=jnp.float32,
-    )
+            jnp.where(ones == 0, 2, jnp.where(ones == tokens_here, 0, 1)),
+            jnp.where(ones == tokens_here, 2, jnp.where(ones == 0, 0, 1)),
+            jnp.min(start),
+            jnp.max(start),
+            col * tokens_here,
+            col * tokens_here + tokens_here - 1,
+        ]
+    ).astype(jnp.int32)
+    mixed = attention(
+        facts,
+        page_table,
+        q,
+        kv.reshape(32 * tokens_here, 512),
+        pool,
+        start[None],
+        index[None],
+        group[None],
+    )
+    projected = jnp.dot(mixed, w_out_all, preferred_element_type=jnp.float32)
     mid = (hidden_in.astype(jnp.float32) + projected).astype(jnp.bfloat16)
     moe_in = root_mean_scale(mid, moe_gain).astype(jnp.bfloat16)
     moe = experts(moe_in, expert_ids, gate_weights, w_gate_up[0], w_down[0])

time: 602 us -> 341 us (0.57)
  waiting for transfers between devices: 300 us -> 33.7 us
  Pallas kernels: 156 us -> 261 us
  matrix products: 72.9 us -> 4.96 us
  other arithmetic: 35.6 us -> 15.4 us
  local copies, waits for them, and re-layouts: 23.1 us -> 7.15 us
    all_gather x5 -> x2, waiting for transfers between devices: 299 us -> 33 us  [the longest x1 33 us: local(): w_out_all = lax.all_gather(w_out, 'expert', axis=0, tiled=True)]
    pallas_call x0 -> x2, Pallas kernels: none -> 105 us  [the longest x1 90 us: front(): pl.pallas_call(front_kernel, out_shape=(jax.ShapeDtypeStruct((2, 8 * toke...]
    dot_general x6 -> x1, matrix products: 72.9 us -> 4.96 us  [local(): projected = jnp.dot(mixed, w_out_all, preferred_element_type=jnp.float32)]
    reduce_sum x9 -> x1, other arithmetic: 26.5 us -> 3.75 us  [local(): ones = jnp.sum(group)]
    slice x5 -> x2, local copies, waits for them, and re-layouts: 9.17 us -> 1.33 us  [the longest x1 0.67 us: local(): ends.append(ends[-1] + lengths_row[r])]
    unnamed x19 -> x8, local copies, waits for them, and re-layouts: 9.49 us -> 3.13 us
  transfers between devices with their start and end apart: 5 -> 2, of which waited for: 5 -> 1; matrix products, arithmetic and copies ran while one was open for 20% -> 5% of each run, Pallas kernels for 0% -> 31%
where the time goes in v2:
time: 341 us; the launch traced here: 340 us
  Pallas kernels  261 us (77%)
  waiting for transfers between devices  33.7 us (10%)
  between operations  17.4 us (5%)
  other arithmetic  15.4 us (5%)
  local copies, waits for them, and re-layouts  7.15 us (2%)
  matrix products  4.96 us (1%)
    pallas_call x1, Pallas kernels, experts(): pl.pallas_call(moe_kernel, out_shape=jax.ShapeDtypeStruct((tokens, width)...  156 us
    pallas_call x1, Pallas kernels, front(): pl.pallas_call(front_kernel, out_shape=(jax.ShapeDtypeStruct((2, 8 * toke...  90 us
    all_gather x1, waiting for transfers between devices, local(): w_out_all = lax.all_gather(w_out, 'expert', axis=0, tiled=True)  33 us
    pallas_call x1, Pallas kernels, attention(): pl.pallas_call(attention_kernel, out_shape=jax.ShapeDtypeStruct((tokens,...  15.5 us
  transfers between devices with their start and end apart: 2, of which 1 were waited for; matrix products, arithmetic and copies ran while one was open for 5% of the time, Pallas kernels for 31%

profile of v2, /device:TPU:1, one launch (start us, length us, event | category | flops | bytes accessed | tf_op | source)
XLA Modules:
  0.0 340.0 jit_solution(4005980305985691086)
XLA Ops:
  7.2 0.0 all-gather.3.cloned.1.call-start
  7.2 2.5 copy.20
  9.7 0.0 all-gather.3.cloned.1.call-update
  9.7 0.0 all-gather.5.cloned.1.call-start
  9.7 0.7 all-gather.5.cloned.1.call-update
  10.5 0.7 constant_dynamic-slice_fusion
  11.2 0.7 fusion.5
  13.8 0.7 fusion.6
  14.5 3.8 %fusion.3 = s32[]{:T(128)} fusion(s32[]{:T(128)} %bitcast.6, s32[]{:T(128)} %bitcast.5, s32[]{:T(128)} %bitcast, s32[]{:T(128)} %bitcast.4, s32[]{:T(128)S(6)} %add.79, s32[]{:T(128)} %bitcast.3, s32[]{:T(128)S(6)} %add.80, s32[]{:T(128)} %mul.18), kind=kLoop, calls=%fused_computation.24 | loop fusion | flops 1023 | bytes 36 | tf_op jit(solution)/shard_map/reduce_sum | solution.py:777
  19.6 0.7 add_convert_fusion.1
  20.3 0.3 fusion.2
  20.6 0.7 pad_maximum_fusion.cos_ref
  21.3 0.7 pad_maximum_fusion.1.sin_ref
  22.0 90.0 %shard_map.158 = (bf16[2,1024,128]{2,1,0:T(8,128)(2,1)}, bf16[4,2,4,128,512]{4,3,2,1,0:T(8,128)(2,1)}, bf16[128,512]{1,0:T(8,128)(2,1)}) custom-call(bf16[128,2048]{1,0:T(8,128)(2,1)} %hidden_ref.1, f32[1,2048]{1,0:T(1,128)} %bitcast.29, bf16[64,2560]{1,0:T(8,128)(2,1)} %shard_ref.1, f32[1,128]{1,0:T(1,128)} %bitcast.32, f32[1,128]{1,0:T(1,128)} %bitcast.33, ...), custom_call_target="tpu_custom_call" | custom-call | flops 1400000000 | bytes 200000000 | tf_op jit(solution)/shard_map/pallas_call | solution.py:593
  112.0 0.6 fusion.4
  112.7 2.0 stack.27.facts
  114.6 3.7 %compare_select_fusion.4.group_ref = s32[1,128]{1,0:T(1,128)} fusion(s32[]{:T(128)} %bitcast.6, s32[]{:T(128)} %bitcast.5, s32[]{:T(128)} %bitcast.4, s32[]{:T(128)} %bitcast.3, s32[]{:T(128)} %bitcast, s32[]{:T(128)S(6)} %add.79, s32[]{:T(128)S(6)} %add.80, s32[]{:T(128)} %mul.18), kind=kLoop, calls=%fused_computation.16 | loop fusion | flops 896 | bytes 544 | tf_op jit(solution)/shard_map/jit(_where)/select_n | solution.py:762
  118.3 1.2 compare_select_fusion.5.start_ref
  119.5 0.6 iota_add_fusion.index_ref
  120.1 0.0 all-gather.3.cloned.1.call-done.pool_ref
  120.1 0.0 copy-start
  120.1 15.5 %shard_map.159 = bf16[128,2048]{1,0:T(8,128)(2,1)} custom-call(s32[6]{0:T(128)} %stack.27.facts, s32[32]{0:T(128)} %table.1, bf16[2,1024,128]{2,1,0:T(8,128)(2,1)} %get-tuple-element.5.q_ref, bf16[4096,512]{1,0:T(8,128)(2,1)} %bitcast.34, bf16[32,2,2,128,128]{4,3,2,1,0:T(8,128)(2,1)} %all-gather.3.cloned.1.call-done.pool_ref, ...), custom_call_target="tpu_custom_call" | custom-call | flops 5000000000 | bytes 10000000 | tf_op jit(solution)/shard_map/pallas_call | solution.py:712
  135.6 0.0 copy-start.2
  135.6 33.0 %all-gather.5.cloned.1.call-done = bf16[2048,2048]{1,0:T(8,128)(2,1)} async-done(((bf16[64,2048]{1,0:T(8,128)(2,1)}), bf16[2048,2048]{1,0:T(8,128)(2,1)}) %all-gather.5.cloned.1.call-update) | async-done | bytes 8388624 | tf_op jit(solution)/shard_map/all_gather | solution.py:750
  168.6 0.0 copy-done
  168.6 5.0 %multiply_reduce_fusion = (f32[128]{0:T(128)S(1)}, f32[128,2048]{1,0:T(8,128)S(1)}) fusion(bf16[128,2048]{1,0:T(8,128)(2,1)} %shard_map.159, bf16[2048,2048]{1,0:T(8,128)(2,1)} %all-gather.5.cloned.1.call-done, bf16[128,2048]{1,0:T(8,128)(2,1)S(1)} %copy-done), kind=kOutput, calls=%fused_computation.6 | convolution fusion | flops 1075314560 | bytes 10486272 | tf_op jit(solution)/shard_map/dot_general | solution.py:798
  173.6 0.0 copy-done.2
  173.6 0.9 multiply_convert_fusion.x_ref
  174.6 0.0 copy-start.1
  174.6 155.8 %shard_map.160 = f32[128,2048]{1,0:T(8,128)} custom-call(bf16[128,2048]{1,0:T(8,128)(2,1)} %multiply_convert_fusion.x_ref, s32[8,128]{1,0:T(8,128)} %bitcast.30, f32[8,128]{1,0:T(8,128)} %bitcast.31, bf16[2048,1536]{1,0:T(8,128)(2,1)} %bitcast.27, bf16[768,2048]{1,0:T(8,128)(2,1)} %bitcast.28), custom_call_target="tpu_custom_call" | custom-call | flops 20000000000 | bytes 400000000 | tf_op jit(solution)/shard_map/pallas_call | solution.py:297
  330.3 2.1 add_convert_fusion
  332.5 0.0 copy-done.1
  332.5 0.7 copy.22
  (2 shorter events, 0.0 us)
Async XLA Ops:
  7.2 113.0 %all-gather.3.cloned.1.call-start = ((), (), s32[]{:S(2)}) async-start(), calls=%async_computation | async-start | bytes 5242880 | tf_op jit(solution)/shard_map/all_gather | solution.py:749
  9.7 158.9 %all-gather.5.cloned.1.call-start = ((), (), s32[]{:S(2)}) async-start(), calls=%async_computation.1 | async-start | bytes 8650752 | tf_op jit(solution)/shard_map/all_gather | solution.py:750
  120.1 48.5 %copy-start = (bf16[128,2048]{1,0:T(8,128)(2,1)S(1)}, bf16[128,2048]{1,0:T(8,128)(2,1)}, u32[]{:S(2)}) copy-start(bf16[128,2048]{1,0:T(8,128)(2,1)} %hidden_ref.1) | copy-start | bytes 1572868
  135.6 38.0 %copy-start.2 = (f32[2048]{0:T(1024)S(1)}, f32[2048]{0:T(1024)}, u32[]{:S(2)}) copy-start(f32[2048]{0:T(1024)} %param.21) | copy-start | bytes 24580
  174.6 157.9 %copy-start.1 = (bf16[128,512]{1,0:T(8,128)(2,1)S(1)}, bf16[128,512]{1,0:T(8,128)(2,1)}, u32[]{:S(2)}) copy-start(bf16[128,512]{1,0:T(8,128)(2,1)} %get-tuple-element.29) | copy-start | bytes 393220
Sparse Core Ops, SparseCore 0:
  9.8 50.3 all-gather.2
  63.3 105.3 all-gather.4

commit v3 on v2

--- a/solution.py
+++ b/solution.py
@@ -13,15 +13,6 @@
 eps = 1e-06
 theta = 1000000.0
 floor_value = -1e30
-
-
-def root_mean_scale(value_rows, gain):
-    value_rows = value_rows.astype(jnp.float32)
-    return (
-        value_rows
-        * lax.rsqrt(jnp.mean(value_rows * value_rows, axis=-1, keepdims=True) + eps)
-        * gain
-    )
 
 
 MESH_ID = pl.DeviceIdType.MESH
@@ -100,6 +91,7 @@
 
 def moe_kernel(
     x_ref,
+    mid_ref,
     ids_ref,
     gates_ref,
     gate_up_hbm,
@@ -113,6 +105,7 @@
     back_b,
     home_a,
     home_b,
+    moe_sum,
     gate_up,
     down,
     rows,
@@ -258,7 +251,7 @@
     pltpu.make_async_copy(home_a, home_a, home_sem.at[0]).wait()
     pltpu.make_async_copy(home_b, home_b, home_sem.at[1]).wait()
 
-    out_ref[...] = jnp.zeros_like(out_ref)
+    moe_sum[...] = jnp.zeros_like(moe_sum)
     over_rows = (((0,), (0,)), ((), ()))
 
     def combine(part, _):
@@ -268,7 +261,7 @@
             exact = (choice(part, wanted) * weight).reshape(256, 128)
             coarse = exact.astype(bf16)
             fine = (exact - coarse.astype(f32)).astype(bf16)
-            out_ref[:, columns] += lax.dot_general(
+            moe_sum[:, columns] += lax.dot_general(
                 coarse, values, over_rows, preferred_element_type=f32
             ) + lax.dot_general(fine, values, over_rows, preferred_element_type=f32)
 
@@ -279,6 +272,7 @@
         return 0
 
     lax.fori_loop(0, 4, combine, 0)
+    out_ref[...] = (mid_ref[...].astype(f32) + moe_sum[...]).astype(bf16)
     others = pl.ds(0, 127 * 8)
     pltpu.make_async_copy(send_a.at[others], send_a.at[others], out_sem.at[0]).wait()
     pltpu.make_async_copy(send_b.at[others], send_b.at[others], out_sem.at[1]).wait()
@@ -286,7 +280,7 @@
     pltpu.make_async_copy(back_b.at[others], back_b.at[others], back_sem.at[1]).wait()
 
 
-def experts(moe_in, ids, gates, gate_up, down):
+def experts(moe_in, mid, ids, gates, gate_up, down):
     tokens, width = moe_in.shape
     ff = down.shape[0]
     groups = 128 // CHUNK
@@ -296,8 +290,8 @@
     b_shape = pltpu.VMEM((1024, width // 2), jnp.bfloat16)
     return pl.pallas_call(
         moe_kernel,
-        out_shape=jax.ShapeDtypeStruct((tokens, width), jnp.float32),
-        in_specs=[vmem, vmem, vmem, hbm, hbm],
+        out_shape=jax.ShapeDtypeStruct((tokens, width), jnp.bfloat16),
+        in_specs=[vmem] * 4 + [hbm] * 2,
         out_specs=vmem,
         scratch_shapes=[
             a_shape,
@@ -308,6 +302,7 @@
             b_shape,
             a_shape,
             b_shape,
+            pltpu.VMEM((tokens, width), jnp.float32),
             pltpu.VMEM((width, 2 * ff), jnp.bfloat16),
             pltpu.VMEM((ff, width), jnp.bfloat16),
             pltpu.VMEM((CHUNK * 12, width), jnp.bfloat16),
@@ -328,7 +323,7 @@
         cost_estimate=pl.CostEstimate(
             flops=20_000_000_000, bytes_accessed=400_000_000, transcendentals=1_000_000
         ),
-    )(moe_in, ids.T, gates.T, gate_up, down)
+    )(moe_in, mid, ids.T, gates.T, gate_up, down)
 
 
 def arrived(ref, sem):
@@ -441,28 +436,38 @@
                         arrived(pick(0, h), self.send_sem.at[r, phase, d, h])
 
 
+def request_bounds(lengths_ref, row):
+    ends = [lengths_ref[row, 0]]
+    for r in range(1, 3):
+        ends.append(ends[-1] + lengths_ref[row, r])
+    return ends
+
+
 def front_kernel(
+    lengths_ref,
     hidden_ref,
     gain_ref,
     shard_ref,
+    out_shard_ref,
+    pool_ref,
     q_gain_ref,
     k_gain_ref,
-    cos_ref,
-    sin_ref,
+    freq_ref,
     q_ref,
     kv_ref,
     cache_ref,
+    w_out_ref,
+    pages_ref,
     weight,
     qkv,
     normed_ref,
-    w_send,
-    w_recv,
-    w_cross,
-    k_send,
-    k_recv,
-    k_cross,
-    swap_send,
-    swap_recv,
+    w_sems,
+    k_sems,
+    o_sems,
+    cross_sems,
+    w_swap,
+    o_swap,
+    pool_sems,
     local_sem,
 ):
     f32, bf16 = jnp.float32, jnp.bfloat16
@@ -471,16 +476,18 @@
     own = lax.div(x, 2)
     columns = weight.shape[-1]
     side = columns // 2
-    turn = side // 2
     partner = (x, y, z, 1 - c)
     even = 1 - lax.rem(x, 2)
     across = (lax.rem(x + 1 + 2 * even, 4), y, z, c)
     opposite = (lax.rem(x + 2, 4), y, z, c)
+    upper = (lax.rem(x + 1, 4), y, z, c)
+    lower = (lax.rem(x + 3, 4), y, z, c)
     barrier = pltpu.get_barrier_semaphore()
     peers = (
         partner,
-        across,
         opposite,
+        upper,
+        lower,
         (x, lax.rem(y + 1, 4), z, c),
         (x, lax.rem(y + 3, 4), z, c),
         (x, y, lax.rem(z + 1, 4), c),
@@ -488,50 +495,99 @@
     )
     for peer in peers:
         pl.semaphore_signal(barrier, inc=1, device_id=device(*peer), device_id_type=MESH_ID)
+    out_side = w_out_ref.shape[-1] // 2
     mine = pl.ds(pl.multiple_of(c * side, 128), side)
-    seed = pltpu.make_async_copy(
-        shard_ref.at[:, mine], weight.at[y, own, z, :, mine], local_sem
-    )
-    seed.start()
-    seed.wait()
+    mine_out = pl.ds(pl.multiple_of(c * out_side, 128), out_side)
+    held = pool_ref.shape[0]
+    row = lax.rem(x, 2) * 2 + c
+    seeds = (
+        pltpu.make_async_copy(
+            shard_ref.at[:, mine], weight.at[y, own, z, :, mine], local_sem.at[0]
+        ),
+        pltpu.make_async_copy(
+            out_shard_ref.at[:, mine_out], w_out_ref.at[y, own, z, :, mine_out], local_sem.at[1]
+        ),
+        pltpu.make_async_copy(pool_ref, pages_ref.at[pl.ds(row * held, held)], local_sem.at[2]),
+    )
+    for seed in seeds:
+        seed.start()
+    seeds[0].wait()
     pl.semaphore_wait(barrier, len(peers))
 
     gather = Gather(
         weight,
         here,
         across,
-        ((c * side, turn), (c * side + turn, side - turn)),
-        (w_send, w_recv, w_cross),
+        ((c * side, side // 2), (c * side + side // 2, side // 2)),
+        (w_sems.at[0], w_sems.at[1], cross_sems.at[0]),
     )
     gather.start()
+    seeds[1].wait()
+    seeds[2].wait()
+    project_out = Gather(
+        w_out_ref,
+        here,
+        across,
+        ((c * out_side, out_side // 2), (c * out_side + out_side // 2, out_side // 2)),
+        (o_sems.at[0], o_sems.at[1], cross_sems.at[1]),
+    )
+
+    def pool_send(slot, first, count, there):
+        piece = pages_ref.at[pl.ds(first, count)]
+        copy = send(piece, piece, pool_sems.at[0, slot], pool_sems.at[1, slot], there)
+        copy.start()
+        return copy
+
+    few = held // 2
+    far_row = (1 - lax.rem(x, 2)) * 2 + c
+    pool_copies = [
+        pool_send(0, row * held, few, upper),
+        pool_send(1, row * held + few, few, lower),
+        pool_send(2, row * held, held, partner),
+    ]
 
     value = hidden_ref[...].astype(f32)
     mean = jnp.mean(value * value, axis=-1, keepdims=True)
     normed_ref[...] = (value * lax.rsqrt(mean + eps) * gain_ref[...]).astype(bf16)
 
     gather.first()
-    swaps = []
-
-    def swap(r, slot, piece):
-        copy = send(piece, piece, swap_send.at[r, slot], swap_recv.at[r, slot], partner)
-        copy.start()
-        swaps.append(copy)
-
+
+    def swapper(sems, kept):
+        def swap(r, slot, piece):
+            copy = send(piece, piece, sems.at[0, r, slot], sems.at[1, r, slot], partner)
+            copy.start()
+            kept.append(copy)
+
+        return swap
+
+    def swap_near(target, ref, swap):
+        for r in range(2):
+            pos, _, _ = target.ring(r, 1)
+            cut = target.cut(r)
+            swap(r, 6, ref.at[pos, :, :, :, cut] if r == 0 else ref.at[:, :, pos, :, cut])
+
+    def swap_forwarded(target, swap):
+        for d in range(2):
+            for r in range(2):
+                pos, _, _ = target.ring(r, 1)
+                swap(r, d * 2 + d, target.far(r)(lax.rem(pos + (3, 1)[d], 4), d))
+
+    w_kept, o_kept = [], []
+    w_pair = swapper(w_swap, w_kept)
+    o_pair = swapper(o_swap, o_kept)
     gather.push(1, 0)
     gather.push(1, 1)
-    for r in range(2):
-        pos, _, _ = gather.ring(r, 1)
-        cut = gather.cut(r)
-        whole = weight.at[pos, :, :, :, cut] if r == 0 else weight.at[:, :, pos, :, cut]
-        swap(r, 6, whole)
+    swap_near(gather, weight, w_pair)
+    project_out.start()
     gather.forward(1)
-    for d in range(2):
-        for r in range(2):
-            pos, _, _ = gather.ring(r, 1)
-            swap(r, d * 2 + d, gather.far(r)(lax.rem(pos + (3, 1)[d], 4), d))
-    gather.rest(1, lambda r, d, h, piece: swap(r, d * 2 + h, piece))
-    for copy in swaps:
+    swap_forwarded(gather, w_pair)
+    gather.rest(1, lambda r, d, h, piece: w_pair(r, d * 2 + h, piece))
+    project_out.first()
+    project_out.push(1, 0)
+    project_out.push(1, 1)
+    for copy in w_kept:
         copy.wait_recv()
+    swap_near(project_out, w_out_ref, o_pair)
 
     span = 2 * 4 * weight.shape[3]
 
@@ -548,10 +604,16 @@
         qkv[:, pl.ds(at, 512)] = total
         return 0
 
-    lax.fori_loop(0, columns // 512, project, 0)
-
-    cosine = cos_ref[...]
-    sine = sin_ref[...]
+    tokens = hidden_ref.shape[0]
+    index = (y * 8 + own * 4 + z) * tokens + lax.broadcasted_iota(jnp.int32, (tokens, 128), 0)
+    start = jnp.zeros_like(index)
+    for end in request_bounds(lengths_ref, row):
+        start = jnp.where(index >= end, end, start)
+    angles = (PREFIX_TOKENS + index - start).astype(f32) * freq_ref[...]
+    cosine = jnp.cos(angles)
+    sine = jnp.sin(angles)
+    lane = lax.broadcasted_iota(jnp.int32, (tokens, 128), 1)
+    sine = jnp.where(lane < 64, -sine, sine)
     heads = columns // 128
 
     def turned(head, gain):
@@ -560,58 +622,82 @@
         rows = rows * lax.rsqrt(mean + eps) * gain
         return (rows * cosine + pltpu.roll(rows, 64, 1) * sine).astype(bf16)
 
+    project(columns // 512 - 1, 0)
     for h in range(2):
         cache_ref[:, h * 128 : (h + 1) * 128] = turned(heads - 4 + h, k_gain_ref[...])
     cache_ref[:, 256:512] = qkv[:, columns - 256 :].astype(bf16)
-    seed = pltpu.make_async_copy(cache_ref, kv_ref.at[y, own, z], local_sem)
+    seed = pltpu.make_async_copy(cache_ref, kv_ref.at[y, own, z], local_sem.at[0])
     seed.start()
     seed.wait()
-    spread = Gather(kv_ref, here, opposite, ((0, 256), (256, 256)), (k_send, k_recv, k_cross))
+    spread = Gather(
+        kv_ref,
+        here,
+        opposite,
+        ((0, 256), (256, 256)),
+        (k_sems.at[0], k_sems.at[1], cross_sems.at[2]),
+    )
     spread.start()
+    lax.fori_loop(0, columns // 512 - 1, project, 0)
 
     def query(head, _):
         at = pl.multiple_of(lax.rem(head, 8) * 128, 128)
         q_ref[lax.div(head, 8), pl.ds(at, 128), :] = turned(head, q_gain_ref[...])
         return 0
 
+    spread.first()
+    spread.push(1, 0)
+    spread.push(1, 1)
+    arrived(pages_ref.at[pl.ds(0, few)], pool_sems.at[1, 0])
+    arrived(pages_ref.at[pl.ds(0, few)], pool_sems.at[1, 1])
+    pool_copies.append(pool_send(3, far_row * held, held, partner))
     lax.fori_loop(0, heads - 4, query, 0)
-    spread.first()
-    spread.second()
+    spread.forward(1)
+    project_out.forward(1)
+    swap_forwarded(project_out, o_pair)
+    spread.rest(1, None)
+    project_out.rest(1, lambda r, d, h, piece: o_pair(r, d * 2 + h, piece))
+    for copy in o_kept:
+        copy.wait_recv()
+    for copy in pool_copies[2:]:
+        copy.wait_recv()
     gather.drain()
     spread.drain()
-    for copy in swaps:
+    project_out.drain()
+    for copy in w_kept + o_kept + pool_copies:
         copy.wait_send()
 
 
-def front(hidden, gain, shard, q_gain, k_gain, cosine, sine):
+def front(lengths, hidden, gain, shard, out_shard, pool, q_gain, k_gain, freqs):
     tokens, width = hidden.shape
     rows, columns = shard.shape
     vmem = pl.BlockSpec(memory_space=pltpu.VMEM)
-    ring = pltpu.SemaphoreType.DMA((2, 2, 3, 2))
-    two = pltpu.SemaphoreType.DMA((2,))
-    swap = pltpu.SemaphoreType.DMA((2, 7))
+    smem = pl.BlockSpec(memory_space=pltpu.SMEM)
+    hbm = pl.BlockSpec(memory_space=pl.ANY)
+    ring = pltpu.SemaphoreType.DMA((2, 2, 2, 3, 2))
+    swap = pltpu.SemaphoreType.DMA((2, 2, 7))
     return pl.pallas_call(
         front_kernel,
         out_shape=(
             jax.ShapeDtypeStruct((2, 8 * tokens, 128), jnp.bfloat16),
             jax.ShapeDtypeStruct((4, 2, 4, tokens, 512), jnp.bfloat16),
             jax.ShapeDtypeStruct((tokens, 512), jnp.bfloat16),
+            jax.ShapeDtypeStruct((4, 2, 4) + out_shard.shape, jnp.bfloat16),
+            jax.ShapeDtypeStruct((4 * pool.shape[0],) + pool.shape[1:], jnp.bfloat16),
         ),
-        in_specs=[vmem] * 7,
-        out_specs=(vmem, vmem, vmem),
+        in_specs=[smem] + [vmem] * 8,
+        out_specs=(vmem, hbm, vmem, hbm, hbm),
         scratch_shapes=[
             pltpu.VMEM((4, 2, 4, rows, columns), jnp.bfloat16),
             pltpu.VMEM((tokens, columns), jnp.float32),
             pltpu.VMEM((tokens, width), jnp.bfloat16),
             ring,
             ring,
-            two,
             ring,
-            ring,
-            two,
+            pltpu.SemaphoreType.DMA((3, 2)),
             swap,
             swap,
-            pltpu.SemaphoreType.DMA,
+            pltpu.SemaphoreType.DMA((2, 4)),
+            pltpu.SemaphoreType.DMA((3,)),
         ],
         compiler_params=pltpu.CompilerParams(
             collective_id=1, has_side_effects=True, vmem_limit_bytes=56 * 1024 * 1024
@@ -619,13 +705,60 @@
         cost_estimate=pl.CostEstimate(
             flops=1_400_000_000, bytes_accessed=200_000_000, transcendentals=1_000_000
         ),
-    )(hidden, gain, shard, q_gain, k_gain, cosine, sine)
+    )(lengths, hidden, gain, shard, out_shard, pool, q_gain, k_gain, freqs)
 
 
 def attention_kernel(
-    facts, table, q_ref, kv_ref, pool_ref, start_ref, index_ref, group_ref, out_ref, high, total, acc
+    table,
+    lengths_ref,
+    groups_ref,
+    q_ref,
+    hidden_ref,
+    gain_ref,
+    kv_hbm,
+    pool_hbm,
+    w_out_hbm,
+    mid_ref,
+    moe_ref,
+    kv_ref,
+    pool_ref,
+    w_out_ref,
+    mixed,
+    high,
+    total,
+    acc,
+    sems,
 ):
     f32, bf16 = jnp.float32, jnp.bfloat16
+    loads = (
+        pltpu.make_async_copy(pool_hbm, pool_ref, sems.at[0]),
+        pltpu.make_async_copy(kv_hbm, kv_ref, sems.at[1]),
+        pltpu.make_async_copy(w_out_hbm, w_out_ref, sems.at[2]),
+    )
+    for load in loads:
+        load.start()
+    row = lax.axis_index("dp")
+    first = lax.axis_index("expert") * hidden_ref.shape[0]
+    last = first + hidden_ref.shape[0] - 1
+    index = first + lax.broadcasted_iota(jnp.int32, (1, 128), 1)
+    start = jnp.zeros_like(index)
+    group_of = jnp.zeros_like(index) + groups_ref[row, 0]
+    earliest, latest = jnp.int32(0), jnp.int32(0)
+    begin = jnp.int32(0)
+    counts = [jnp.int32(0), jnp.int32(0)]
+    for r in range(4):
+        end = begin + lengths_ref[row, r]
+        of = groups_ref[row, r]
+        if r > 0:
+            start = jnp.where(index >= begin, begin, start)
+            group_of = jnp.where(index >= begin, of, group_of)
+            earliest = jnp.where(first >= begin, begin, earliest)
+            latest = jnp.where(last >= begin, begin, latest)
+        inside = jnp.maximum(jnp.minimum(end, last + 1) - jnp.maximum(begin, first), 0)
+        counts[0] += jnp.where(of == 0, inside, 0)
+        counts[1] += jnp.where(of == 1, inside, 0)
+        begin = end
+    everyone = last - first + 1
     factor = math.log2(math.e) / math.sqrt(128)
     high[...] = jnp.full_like(high, floor_value)
     total[...] = jnp.zeros_like(total)
@@ -648,6 +781,7 @@
         )
 
     span = 4
+    loads[0].wait()
     for group in range(2):
 
         def pages(seen, group=group):
@@ -661,14 +795,15 @@
 
             lax.fori_loop(0, 16 // span, body, 0)
 
-        @pl.when(facts[group] == 2)
+        @pl.when(counts[group] == everyone)
         def _():
             pages(None)
 
-        @pl.when(facts[group] == 1)
+        @pl.when((counts[group] > 0) & (counts[group] < everyone))
         def _():
-            pages(jnp.broadcast_to(group_ref[...] == group, (span * 128, 128)))
-
+            pages(jnp.broadcast_to(group_of == group, (span * 128, 128)))
+
+    loads[1].wait()
     size = 256
 
     def suffix(tile, masked):
@@ -676,14 +811,14 @@
         seen = None
         if masked:
             place_of = at + lax.broadcasted_iota(jnp.int32, (size, 128), 0)
-            seen = (place_of >= start_ref[...]) & (place_of <= index_ref[...])
+            seen = (place_of >= start) & (place_of <= index)
         for h in range(2):
             keys = kv_ref[pl.ds(at, size), h * 128 : (h + 1) * 128]
             values = kv_ref[pl.ds(at, size), 256 + h * 128 : 256 + (h + 1) * 128]
             step(h, keys, values, seen)
 
     def tiles(tile, _):
-        clear = (tile * size >= facts[3]) & (tile * size + size <= facts[4] + 1)
+        clear = (tile * size >= latest) & (tile * size + size <= first + 1)
 
         @pl.when(clear)
         def _():
@@ -695,35 +830,58 @@
 
         return 0
 
-    lax.fori_loop(lax.div(facts[2], size), lax.div(facts[5], size) + 1, tiles, 0)
+    lax.fori_loop(lax.div(earliest, size), lax.div(last, size) + 1, tiles, 0)
     for h in range(2):
         done = acc[h] / total[h]
         for g in range(8):
             head = h * 8 + g
-            out_ref[:, head * 128 : (head + 1) * 128] = (
+            mixed[:, head * 128 : (head + 1) * 128] = (
                 done[:, g * 128 : (g + 1) * 128].T.astype(bf16)
             )
 
 
-def attention(facts, table, q, kv, pool, start, index, group):
+    loads[2].wait()
+
+    def project(tile, square):
+        at = pl.multiple_of(tile * 512, 512)
+        part = jnp.dot(mixed[...], w_out_ref[:, pl.ds(at, 512)], preferred_element_type=f32)
+        mid = (hidden_ref[:, pl.ds(at, 512)].astype(f32) + part).astype(bf16)
+        mid_ref[:, pl.ds(at, 512)] = mid
+        mid = mid.astype(f32)
+        return square + jnp.sum(mid * mid, axis=-1, keepdims=True)
+
+    width = hidden_ref.shape[1]
+    square = lax.fori_loop(0, width // 512, project, jnp.zeros((hidden_ref.shape[0], 1), f32))
+    factor_of = lax.rsqrt(square / width + eps)
+    moe_ref[...] = (mid_ref[...].astype(f32) * factor_of * gain_ref[...]).astype(bf16)
+
+
+def attention(table, lengths, groups, q, hidden, gain, kv, pool, w_out):
     vmem = pl.BlockSpec(memory_space=pltpu.VMEM)
     smem = pl.BlockSpec(memory_space=pltpu.SMEM)
-    tokens = start.shape[1]
+    hbm = pl.BlockSpec(memory_space=pl.ANY)
+    tokens, width = hidden.shape
+    row = jax.ShapeDtypeStruct((tokens, width), jnp.bfloat16)
     return pl.pallas_call(
         attention_kernel,
-        out_shape=jax.ShapeDtypeStruct((tokens, 16 * 128), jnp.bfloat16),
-        in_specs=[smem, smem] + [vmem] * 6,
-        out_specs=vmem,
+        out_shape=(row, row),
+        in_specs=[smem] * 3 + [vmem] * 3 + [hbm] * 3,
+        out_specs=(vmem, vmem),
         scratch_shapes=[
+            pltpu.VMEM(kv.shape, jnp.bfloat16),
+            pltpu.VMEM(pool.shape, jnp.bfloat16),
+            pltpu.VMEM(w_out.shape, jnp.bfloat16),
+            pltpu.VMEM((tokens, width), jnp.bfloat16),
             pltpu.VMEM((2, 1, 8 * tokens), jnp.float32),
             pltpu.VMEM((2, 1, 8 * tokens), jnp.float32),
             pltpu.VMEM((2, 128, 8 * tokens), jnp.float32),
+            pltpu.SemaphoreType.DMA((3,)),
         ],
         compiler_params=pltpu.CompilerParams(vmem_limit_bytes=56 * 1024 * 1024),
         cost_estimate=pl.CostEstimate(
             flops=5_000_000_000, bytes_accessed=10_000_000, transcendentals=10_000_000
         ),
-    )(facts, table, q, kv, pool, start, index, group)
+    )(table, lengths, groups, q, hidden, gain, kv, pool, w_out)
 
 
 def local(
@@ -744,62 +902,31 @@
     gate_weights,
 ):
     tokens_here, width = hidden_in.shape
-    row = lax.axis_index("dp")
-    col = lax.axis_index("expert")
-    pool = lax.all_gather(kv_pool.transpose(0, 1, 3, 2, 4), "dp", axis=0, tiled=True)
-    w_out_all = lax.all_gather(w_out, "expert", axis=0, tiled=True)
-    index = col * tokens_here + jnp.arange(tokens_here, dtype=jnp.int32)
-    lengths_row = lax.dynamic_index_in_dim(suffix_lengths, row, 0, keepdims=False)
-    groups_row = lax.dynamic_index_in_dim(request_group, row, 0, keepdims=False)
-    ends = [lengths_row[0]]
-    for r in range(1, 4):
-        ends.append(ends[-1] + lengths_row[r])
-    start = jnp.zeros_like(index)
-    group = jnp.full_like(index, 0) + groups_row[0]
-    for r in range(3):
-        later = index >= ends[r]
-        start = jnp.where(later, ends[r], start)
-        group = jnp.where(later, groups_row[r + 1], group)
-    offset = index - start
-    half = 64
+    half = q_gain.shape[0] // 2
     freqs = theta ** (-jnp.arange(half, dtype=jnp.float32) / half)
-    angles = (PREFIX_TOKENS + offset).astype(jnp.float32)[:, None] * freqs[None, :]
-    cosine, sine = jnp.cos(angles), jnp.sin(angles)
-    q, kv, suffix_cache = front(
+    q, kv, suffix_cache, w_out_all, pool = front(
+        suffix_lengths,
         hidden_in,
         attn_gain[None],
         query_key_value_weight,
+        w_out,
+        kv_pool.transpose(0, 1, 3, 2, 4),
         q_gain[None],
         key_norm_gain[None],
-        jnp.concatenate([cosine, cosine], axis=1),
-        jnp.concatenate([-sine, sine], axis=1),
-    )
-    ones = jnp.sum(group)
-    facts = jnp.stack(
-        [
-            jnp.where(ones == 0, 2, jnp.where(ones == tokens_here, 0, 1)),
-            jnp.where(ones == tokens_here, 2, jnp.where(ones == 0, 0, 1)),
-            jnp.min(start),
-            jnp.max(start),
-            col * tokens_here,
-            col * tokens_here + tokens_here - 1,
-        ]
-    ).astype(jnp.int32)
-    mixed = attention(
-        facts,
+        jnp.concatenate([freqs, freqs])[None],
+    )
+    mid, moe_in = attention(
         page_table,
+        suffix_lengths,
+        request_group,
         q,
+        hidden_in,
+        moe_gain[None],
         kv.reshape(32 * tokens_here, 512),
         pool,
-        start[None],
-        index[None],
-        group[None],
-    )
-    projected = jnp.dot(mixed, w_out_all, preferred_element_type=jnp.float32)
-    mid = (hidden_in.astype(jnp.float32) + projected).astype(jnp.bfloat16)
-    moe_in = root_mean_scale(mid, moe_gain).astype(jnp.bfloat16)
-    moe = experts(moe_in, expert_ids, gate_weights, w_gate_up[0], w_down[0])
-    hidden_out = (mid.astype(jnp.float32) + moe).astype(jnp.bfloat16)
+        w_out_all.reshape(32 * w_out.shape[0], width),
+    )
+    hidden_out = experts(moe_in, mid, expert_ids, gate_weights, w_gate_up[0], w_down[0])
     return (hidden_out, suffix_cache)
 
 

time: 341 us -> 308 us (0.903)
  Pallas kernels: 261 us -> 298 us
  waiting for transfers between devices: 33.7 us -> 0 us
  between operations: 17.4 us -> 0.67 us
  other arithmetic: 15.4 us -> 0.6 us
  matrix products: 4.96 us -> 0 us
    all_gather x2 -> x0, waiting for transfers between devices: 33 us -> none  [the longest x1 33 us: local(): w_out_all = lax.all_gather(w_out, 'expert', axis=0, tiled=True)]
    pallas_call x1, Pallas kernels: 156 us -> 181 us  [experts(): pl.pallas_call(moe_kernel, out_shape=jax.ShapeDtypeStruct((tokens, width)...]
    pallas_call x1, Pallas kernels: 90 us -> 100 us  [front(): pl.pallas_call(front_kernel, out_shape=(jax.ShapeDtypeStruct((2, 8 * toke...]
    dot_general x1 -> x0, matrix products: 4.96 us -> none  [local(): projected = jnp.dot(mixed, w_out_all, preferred_element_type=jnp.float32)]
    select_n x2 -> x0, other arithmetic: 4.9 us -> none  [the longest x1 3.7 us: local(): group = jnp.where(later, groups_row[r + 1], group)]
    convert_element_type x3 -> x0, other arithmetic: 3.78 us -> none  [the longest x1 2.14 us: local(): hidden_out = (mid.astype(jnp.float32) + moe).astype(jnp.bfloat16)]
    reduce_sum x1 -> x0, other arithmetic: 3.75 us -> none  [local(): ones = jnp.sum(group)]
  transfers between devices with their start and end apart: 2 -> 0, of which waited for: 1 -> 0; matrix products, arithmetic and copies ran while one was open for 5% -> 0% of each run, Pallas kernels for 31% -> 0%
where the time goes in v3:
time: 308 us; the launch traced here: 304 us
  Pallas kernels  298 us (97%)
  local copies, waits for them, and re-layouts  5 us (2%)
    pallas_call x1, Pallas kernels, experts(): pl.pallas_call(moe_kernel, out_shape=jax.ShapeDtypeStruct((tokens, width)...  181 us
    pallas_call x1, Pallas kernels, front(): pl.pallas_call(front_kernel, out_shape=(jax.ShapeDtypeStruct((2, 8 * toke...  100 us
    pallas_call x1, Pallas kernels, attention(): pl.pallas_call(attention_kernel, out_shape=(row, row), in_specs=[smem] *...  16.6 us

profile of v3, /device:TPU:1, one launch (start us, length us, event | category | flops | bytes accessed | tf_op | source)
XLA Modules:
  0.0 304.5 jit_solution(7932604605736368736)
XLA Ops:
  0.6 0.6 maximum_bitcast_fusion.freq_ref
  1.2 2.5 copy.19
  3.7 100.2 %shard_map.158 = (bf16[2,1024,128]{2,1,0:T(8,128)(2,1)}, bf16[4,2,4,128,512]{4,3,2,1,0:T(8,128)(2,1)}, bf16[128,512]{1,0:T(8,128)(2,1)}, bf16[4,2,4,64,2048]{4,3...) custom-call(s32[4,4]{1,0:T(4,128)} %lengths_ref.3, bf16[128,2048]{1,0:T(8,128)(2,1)} %hidden_ref.3, f32[1,2048]{1,0:T(1,128)} %bitcast.18, ...), custom_call_target="tpu_custom_call" | custom-call | flops 1400000000 | bytes 200000000 | tf_op jit(solution)/shard_map/pallas_call | solution.py:678
  103.9 16.6 %shard_map.159 = (bf16[128,2048]{1,0:T(8,128)(2,1)}, bf16[128,2048]{1,0:T(8,128)(2,1)}) custom-call(s32[32]{0:T(128)} %table.1, s32[4,4]{1,0:T(4,128)} %lengths_ref.3, s32[4,4]{1,0:T(4,128)} %groups_ref.1, bf16[2,1024,128]{2,1,0:T(8,128)(2,1)} %get-tuple-element.9.q_ref, bf16[128,2048]{1,0:T(8,128)(2,1)} %hidden_ref.3, f32[1,2048]{1,0:T(1,128)} %bitcast.19, ...), custom_call_target="tpu_custom_call" | custom-call | flops 5000000000 | bytes 10000000 | tf_op jit(solution)/shard_map/pallas_call | solution.py:865
  120.5 0.0 copy-start
  120.5 181.4 %shard_map.160 = bf16[128,2048]{1,0:T(8,128)(2,1)} custom-call(bf16[128,2048]{1,0:T(8,128)(2,1)} %get-tuple-element.13.x_ref, bf16[128,2048]{1,0:T(8,128)(2,1)} %get-tuple-element.14.mid_ref, s32[8,128]{1,0:T(8,128)} %bitcast.20, f32[8,128]{1,0:T(8,128)} %bitcast.21, bf16[2048,1536]{1,0:T(8,128)(2,1)} %bitcast.16, bf16[768,2048]{1,0:T(8,128)(2,1)} %bitcast.17), custom_call_target="tpu_custom_call" | custom-call | flops 20000000000 | bytes 400000000 | tf_op jit(solution)/shard_map/pallas_call | solution.py:291
  301.9 1.9 copy.22
  303.8 0.0 copy-done
  303.8 0.7 copy.23
  (1 shorter events, 0.0 us)
Async XLA Ops:
  120.5 183.3 %copy-start = (bf16[128,512]{1,0:T(8,128)(2,1)S(1)}, bf16[128,512]{1,0:T(8,128)(2,1)}, u32[]{:S(2)}) copy-start(bf16[128,512]{1,0:T(8,128)(2,1)} %get-tuple-element.19) | copy-start | bytes 393220

commit v4 on v3

--- a/solution.py
+++ b/solution.py
@@ -17,7 +17,7 @@
 
 MESH_ID = pl.DeviceIdType.MESH
 STEP = 45
-CHUNK = 16
+PARTS = (0, 640, 1280, 2048)
 
 
 def place():
@@ -35,43 +35,18 @@
     return (lax.rem(x, 2) * 2 + c) * 32 + y * 8 + lax.div(x, 2) * 4 + z
 
 
-def shift(k):
-    o = lax.rem(k * STEP, 128)
-    return (lax.div(o, 32), lax.rem(lax.div(o, 8), 4), lax.rem(lax.div(o, 2), 4), lax.rem(o, 2))
-
-
-def target(here, k):
-    x, y, z, c = here
-    dx, dy, dz, dc = shift(k)
-    sign = 1 - 2 * c
-    return (
-        lax.rem(x + sign * dx + 4, 4),
-        lax.rem(y + sign * dy + 4, 4),
-        lax.rem(z + sign * dz + 4, 4),
-        lax.rem(c + dc, 2),
-    )
-
-
-def origin(here, k):
-    x, y, z, c = here
-    dx, dy, dz, dc = shift(k)
-    source_core = lax.rem(c + dc, 2)
-    sign = 1 - 2 * source_core
-    return (
-        lax.rem(x - sign * dx + 4, 4),
-        lax.rem(y - sign * dy + 4, 4),
-        lax.rem(z - sign * dz + 4, 4),
-        source_core,
-    )
-
-
 def greet_all(here):
     barrier = pltpu.get_barrier_semaphore()
+    x, y, z, c = here
 
     def tell(k, _):
-        pl.semaphore_signal(
-            barrier, inc=1, device_id=device(*target(here, k)), device_id_type=MESH_ID
+        there = (
+            lax.rem(x + lax.div(k, 32), 4),
+            lax.rem(y + lax.rem(lax.div(k, 8), 4), 4),
+            lax.rem(z + lax.rem(lax.div(k, 2), 4), 4),
+            lax.rem(c + k, 2),
         )
+        pl.semaphore_signal(barrier, inc=1, device_id=device(*there), device_id_type=MESH_ID)
         return 0
 
     lax.fori_loop(1, 128, tell, 0)
@@ -89,211 +64,353 @@
     )
 
 
+def part_columns(p):
+    return slice(PARTS[p], PARTS[p + 1])
+
+
+def in_plane(p, here):
+    x, y, z, c = here
+    return ((y, z), (z, x), (y, x))[p]
+
+
+def at_plane(p, here, a, b, c):
+    x, y, z, _ = here
+    return ((x, a, b, c), (b, y, a, c), (b, a, z, c))[p]
+
+
+def on_line(p, here, d):
+    moved = list(here)
+    moved[p] = lax.rem(here[p] + d, 4)
+    return tuple(moved)
+
+
 def moe_kernel(
     x_ref,
     mid_ref,
-    ids_ref,
-    gates_ref,
+    info_ref,
     gate_up_hbm,
     down_hbm,
     out_ref,
-    send_a,
-    send_b,
+    line,
+    infos,
+    pack_a,
+    pack_b,
     recv_a,
     recv_b,
-    back_a,
-    back_b,
     home_a,
     home_b,
-    moe_sum,
-    gate_up,
-    down,
     rows,
     acts,
     result,
-    rank_ref,
-    gate_ref,
+    partial,
+    inbox,
+    ranks,
+    gates,
+    gate_up,
+    down,
     weight_sem,
+    line_send,
+    line_recv,
+    info_send,
+    info_recv,
     out_sem,
-    in_a_sem,
-    in_b_sem,
+    in_sem,
     back_sem,
     home_sem,
+    sum_send,
+    sum_recv,
 ):
     f32, bf16 = jnp.float32, jnp.bfloat16
-    width = x_ref.shape[1]
-    half = width // 2
     ff = down.shape[0]
     here = place()
-    me = number(*here)
+    c = here[3]
     load_gate_up = pltpu.make_async_copy(gate_up_hbm, gate_up, weight_sem.at[0])
     load_down = pltpu.make_async_copy(down_hbm, down, weight_sem.at[1])
     load_gate_up.start()
     load_down.start()
     barrier = greet_all(here)
-
-    expert = lax.broadcasted_iota(jnp.int32, (128, 128), 0)
-    token = lax.broadcasted_iota(jnp.int32, (128, 128), 1)
-    named = jnp.zeros((128, 128), f32)
-    gates = jnp.zeros((128, 128), f32)
-    for k in range(ids_ref.shape[0]):
-        hit = ids_ref[k : k + 1, :] == expert
-        named += jnp.where(hit, 1.0, 0.0)
-        gates += jnp.where(hit, gates_ref[k : k + 1, :], 0.0)
-    before = jnp.where(expert < token, 1.0, 0.0).astype(bf16)
-    rank = jnp.dot(named.astype(bf16), before, preferred_element_type=f32)
-    rank_ref[...] = jnp.where(named > 0.5, rank, -1.0)
-    gate_ref[...] = gates
-
-    slot = lax.broadcasted_iota(jnp.int32, (32, 8, 128), 1)
-
-    def choice(part, wanted):
-        ranks = rank_ref[pl.ds(part * 32, 32), :]
-        return jnp.where(ranks[:, None, :] == wanted.astype(f32), 1.0, 0.0)
-
-    def pack(part, _):
-        first = choice(part, slot).reshape(256, 128).astype(bf16)
-        send_a[pl.ds(part * 256, 256), :] = jnp.dot(
-            first, x_ref[...], preferred_element_type=f32
-        ).astype(bf16)
-        low = choice(part, jnp.where(slot < 4, slot + 8, 99)).reshape(256, 128).astype(bf16)
-        high = choice(part, jnp.where(slot >= 4, slot + 4, 99)).reshape(256, 128).astype(bf16)
-        mixed = jnp.dot(low, x_ref[:, :half], preferred_element_type=f32)
-        mixed += jnp.dot(high, x_ref[:, half:], preferred_element_type=f32)
-        send_b[pl.ds(part * 256, 256), :] = mixed.astype(bf16)
-        return 0
-
-    lax.fori_loop(0, 4, pack, 0)
     pl.semaphore_wait(barrier, 127)
 
-    def piece(ref, index):
-        return ref.at[pl.ds(index * 8, 8), :]
-
-    def dispatch(k, _):
-        there = target(here, k)
-        to = number(*there)
-        group = lax.div(k, CHUNK)
-        send(piece(send_a, to), piece(recv_a, k), out_sem.at[0], in_a_sem.at[group], there).start()
-        send(piece(send_b, to), piece(recv_b, k), out_sem.at[1], in_b_sem.at[group], there).start()
-        return 0
-
-    own_a = pltpu.make_async_copy(piece(send_a, me), piece(recv_a, 0), in_a_sem.at[0])
-    own_b = pltpu.make_async_copy(piece(send_b, me), piece(recv_b, 0), in_b_sem.at[0])
-    own_a.start()
-    own_b.start()
-    lax.fori_loop(1, 128, dispatch, 0)
+    for p in range(3):
+        own = here[p]
+        pltpu.make_async_copy(info_ref, infos.at[p, own], info_recv.at[p]).start()
+        for d in (1, 3, 2):
+            send(
+                info_ref, infos.at[p, own], info_send.at[p], info_recv.at[p], on_line(p, here, d)
+            ).start()
+    for d in (1, 3, 2):
+        for p in range(3):
+            cut = part_columns(p)
+            send(
+                x_ref.at[:, cut],
+                line.at[here[p], :, cut],
+                line_send.at[p],
+                line_recv.at[p],
+                on_line(p, here, d),
+            ).start()
+    for p in range(3):
+        cut = part_columns(p)
+        pltpu.make_async_copy(
+            x_ref.at[:, cut], line.at[here[p], :, cut], line_recv.at[p]
+        ).start()
+
+    local = lax.broadcasted_iota(jnp.int32, (32, 128), 0)
+    before = jnp.where(
+        lax.broadcasted_iota(jnp.int32, (128, 128), 0)
+        < lax.broadcasted_iota(jnp.int32, (128, 128), 1),
+        1.0,
+        0.0,
+    ).astype(bf16)
+    for p in range(3):
+        arrived(infos.at[p], info_recv.at[p])
+        expert = number(
+            *at_plane(
+                p,
+                here,
+                lax.rem(lax.div(local, 4), 4),
+                lax.rem(local, 4),
+                lax.div(local, 16),
+            )
+        ).astype(f32)
+        for q in range(4):
+            named = jnp.zeros((32, 128), f32)
+            gate = jnp.zeros((32, 128), f32)
+            for k in range(8):
+                hit = infos[p, q, k : k + 1, :] == expert
+                named += jnp.where(hit, 1.0, 0.0)
+                gate += jnp.where(hit, infos[p, q, 8 + k : 9 + k, :], 0.0)
+            rank = jnp.dot(named.astype(bf16), before, preferred_element_type=f32)
+            ranks[p, :, q * 128 : (q + 1) * 128] = jnp.where(named > 0.5, rank, 99.0)
+            gates[p, :, q * 128 : (q + 1) * 128] = gate
+
+    quarter = lax.div(lax.broadcasted_iota(jnp.int32, (1, 512), 1), 128).astype(f32)
+
+    def choice(p, group, low, count):
+        many = 256 // (4 * count)
+        rank = ranks[p, pl.ds(group * many, many), :]
+        rank = jnp.where(
+            (rank >= low) & (rank < low + count), rank - low + count * quarter, -1.0
+        )
+        wanted = lax.broadcasted_iota(jnp.int32, (many, 4 * count, 512), 1).astype(f32)
+        return jnp.where(rank[:, None, :] == wanted, 1.0, 0.0)
+
+    halves = ((0, 8, pack_a, recv_a, home_a), (8, 4, pack_b, recv_b, home_b))
+
+    def pack(half):
+        low, count, packed, _, _ = halves[half]
+
+        def body(group, _):
+            for p in range(3):
+                cut = part_columns(p)
+                chosen = choice(p, group, low, count).reshape(256, 512).astype(bf16)
+                values = line[:, :, cut].reshape(512, cut.stop - cut.start)
+                packed[pl.ds(group * 256, 256), cut] = jnp.dot(
+                    chosen, values, preferred_element_type=f32
+                ).astype(bf16)
+            return 0
+
+        lax.fori_loop(0, count // 2, body, 0)
+
+    def block(ref, index, size, p):
+        return ref.at[pl.ds(index * size, size), part_columns(p)]
+
+    def exchange(src, dst, size, send_sem, recv_sem):
+        sign = 1 - 2 * c
+
+        def body(k, _):
+            o = lax.rem(k * STEP, 32)
+            for p in range(3):
+                a, b = in_plane(p, here)
+                to_a = lax.rem(a + sign * lax.rem(lax.div(o, 4), 4) + 4, 4)
+                to_b = lax.rem(b + sign * lax.rem(o, 4) + 4, 4)
+                to_c = lax.rem(c + lax.div(o, 16), 2)
+                send(
+                    block(src, to_c * 16 + to_a * 4 + to_b, size, p),
+                    block(dst, c * 16 + a * 4 + b, size, p),
+                    send_sem.at[p],
+                    recv_sem.at[p],
+                    at_plane(p, here, to_a, to_b, to_c),
+                ).start()
+            return 0
+
+        lax.fori_loop(1, 32, body, 0)
+        for p in range(3):
+            a, b = in_plane(p, here)
+            index = c * 16 + a * 4 + b
+            pltpu.make_async_copy(
+                block(src, index, size, p), block(dst, index, size, p), recv_sem.at[p]
+            ).start()
+
+    for p in range(3):
+        cut = part_columns(p)
+        arrived(line.at[:, :, cut], line_recv.at[p])
+    for half in range(2):
+        low, count, packed, received, _ = halves[half]
+        pack(half)
+        exchange(packed, received, 4 * count, out_sem.at[half], in_sem.at[half])
     load_gate_up.wait()
     load_down.wait()
 
-    tall, short = CHUNK * 8, CHUNK * 4
-    row = lax.broadcasted_iota(jnp.int32, (short, tall), 0)
-    column = lax.broadcasted_iota(jnp.int32, (short, tall), 1)
-    at_low = lax.div(row, 4) * 8 + lax.rem(row, 4)
-    take_low = jnp.where(column == at_low, 1.0, 0.0).astype(bf16)
-    take_high = jnp.where(column == at_low + 4, 1.0, 0.0).astype(bf16)
-    row_t = lax.broadcasted_iota(jnp.int32, (tall, short), 0)
-    column_t = lax.broadcasted_iota(jnp.int32, (tall, short), 1)
-    at_low_t = lax.div(column_t, 4) * 8 + lax.rem(column_t, 4)
-    give_low = jnp.where(row_t == at_low_t, 1.0, 0.0).astype(bf16)
-    give_high = jnp.where(row_t == at_low_t + 4, 1.0, 0.0).astype(bf16)
-
-    def work(group, _):
-        a_rows = recv_a.at[pl.ds(group * tall, tall), :]
-        b_rows = recv_b.at[pl.ds(group * tall, tall), :]
-        pltpu.make_async_copy(a_rows, a_rows, in_a_sem.at[group]).wait()
-        pltpu.make_async_copy(b_rows, b_rows, in_b_sem.at[group]).wait()
-        rows[:tall, :] = a_rows[...]
-        rows[tall:, :half] = jnp.dot(
-            take_low, b_rows[...], preferred_element_type=f32
-        ).astype(bf16)
-        rows[tall:, half:] = jnp.dot(
-            take_high, b_rows[...], preferred_element_type=f32
-        ).astype(bf16)
+    def swapped(count):
+        size = 16 * count
+        row = lax.broadcasted_iota(jnp.int32, (size, size), 0)
+        column = lax.broadcasted_iota(jnp.int32, (size, size), 1)
+        source = (
+            lax.rem(lax.div(row, count), 4) * 4 * count
+            + lax.div(row, 4 * count) * count
+            + lax.rem(row, count)
+        )
+        return jnp.where(column == source, 1.0, 0.0).astype(bf16)
+
+    def others(ref, size, p):
+        return ref.at[pl.ds(0, 31 * size), part_columns(p)]
+
+    for half in range(2):
+        low, count, packed, received, home = halves[half]
+        size = 4 * count
+        total = 32 * size
+        for p in range(3):
+            arrived(received.at[:, part_columns(p)], in_sem.at[half, p])
+        turn = swapped(count)
+        rows[:total, part_columns(0)] = received[:, part_columns(0)]
+
+        def unpack(group, _):
+            core, a = lax.div(group, 4), lax.rem(group, 4)
+            cut = part_columns(1)
+            block_y = jnp.dot(
+                turn, received[pl.ds(group * 4 * size, 4 * size), cut], preferred_element_type=f32
+            ).astype(bf16)
+            for y in range(4):
+                at = (core * 16 + y * 4 + a) * size
+                rows[pl.ds(pl.multiple_of(at, size), size), cut] = block_y[
+                    y * size : (y + 1) * size
+                ]
+            cut = part_columns(2)
+            rows[pl.ds(group * 4 * size, 4 * size), cut] = jnp.dot(
+                turn, received[pl.ds(group * 4 * size, 4 * size), cut], preferred_element_type=f32
+            ).astype(bf16)
+            return 0
+
+        lax.fori_loop(0, 8, unpack, 0)
 
         def up(tile, _):
             at = pl.multiple_of(tile * 256, 256)
-            first = jnp.dot(rows[...], gate_up[:, pl.ds(at, 256)], preferred_element_type=f32)
-            second = jnp.dot(
-                rows[...], gate_up[:, pl.ds(ff + at, 256)], preferred_element_type=f32
-            )
-            acts[:, pl.ds(at, 256)] = (jax.nn.silu(first) * second).astype(bf16)
+            values = rows[:total, :]
+            first = jnp.dot(values, gate_up[:, pl.ds(at, 256)], preferred_element_type=f32)
+            second = jnp.dot(values, gate_up[:, pl.ds(ff + at, 256)], preferred_element_type=f32)
+            acts[:total, pl.ds(at, 256)] = (jax.nn.silu(first) * second).astype(bf16)
             return 0
 
         lax.fori_loop(0, ff // 256, up, 0)
-
-        def lower(tile, _):
-            at = pl.multiple_of(tile * 512, 512)
-            result[:, pl.ds(at, 512)] = jnp.dot(
-                acts[...], down[:, pl.ds(at, 512)], preferred_element_type=f32
+        for p in range(3):
+            arrived(others(packed, size, p), out_sem.at[half, p])
+
+        def lower(group, _):
+            at = pl.multiple_of(group * 256, 256)
+            for p in range(3):
+                cut = part_columns(p)
+                value = jnp.dot(
+                    acts[pl.ds(at, 256), :], down[:, cut], preferred_element_type=f32
+                ).astype(bf16)
+                if p == 0:
+                    packed[pl.ds(at, 256), cut] = value
+                else:
+                    result[pl.ds(at, 256), cut.start - PARTS[1] : cut.stop - PARTS[1]] = value
+            return 0
+
+        lax.fori_loop(0, total // 256, lower, 0)
+
+        def repack(group, _):
+            core, a = lax.div(group, 4), lax.rem(group, 4)
+            cut = slice(0, PARTS[2] - PARTS[1])
+            pieces = []
+            for y in range(4):
+                at = (core * 16 + y * 4 + a) * size
+                pieces.append(result[pl.ds(pl.multiple_of(at, size), size), cut])
+            packed[pl.ds(group * 4 * size, 4 * size), part_columns(1)] = jnp.dot(
+                turn, jnp.concatenate(pieces, axis=0), preferred_element_type=f32
+            ).astype(bf16)
+            cut = slice(PARTS[2] - PARTS[1], PARTS[3] - PARTS[1])
+            packed[pl.ds(group * 4 * size, 4 * size), part_columns(2)] = jnp.dot(
+                turn, result[pl.ds(group * 4 * size, 4 * size), cut], preferred_element_type=f32
             ).astype(bf16)
             return 0
 
-        lax.fori_loop(0, width // 512, lower, 0)
-        back_a[pl.ds(group * tall, tall), :] = result[:tall, :]
-        mixed = jnp.dot(give_low, result[tall:, :half], preferred_element_type=f32)
-        mixed += jnp.dot(give_high, result[tall:, half:], preferred_element_type=f32)
-        back_b[pl.ds(group * tall, tall), :] = mixed.astype(bf16)
-
-        def give(k, _):
-            there = origin(here, k)
-            send(piece(back_a, k), piece(home_a, me), back_sem.at[0], home_sem.at[0], there).start()
-            send(piece(back_b, k), piece(home_b, me), back_sem.at[1], home_sem.at[1], there).start()
+        lax.fori_loop(0, 8, repack, 0)
+        exchange(packed, home, size, back_sem.at[half], home_sem.at[half])
+
+    partial[...] = jnp.zeros_like(partial)
+    over_rows = (((0,), (0,)), ((), ()))
+    for half in range(2):
+        low, count, packed, received, home = halves[half]
+        many = 256 // (4 * count)
+        for p in range(3):
+            arrived(home.at[:, part_columns(p)], home_sem.at[half, p])
+
+        def combine(group, _):
+            for p in range(3):
+                cut = part_columns(p)
+                gate = gates[p, pl.ds(group * many, many), :]
+                exact = (choice(p, group, low, count) * gate[:, None, :]).reshape(256, 512)
+                coarse = exact.astype(bf16)
+                fine = (exact - coarse.astype(f32)).astype(bf16)
+                values = home[pl.ds(group * 256, 256), cut]
+                partial[:, cut] += lax.dot_general(
+                    coarse, values, over_rows, preferred_element_type=f32
+                ) + lax.dot_general(fine, values, over_rows, preferred_element_type=f32)
             return 0
 
-        lax.fori_loop(jnp.where(group == 0, 1, group * CHUNK), (group + 1) * CHUNK, give, 0)
-        return 0
-
-    lax.fori_loop(0, 128 // CHUNK, work, 0)
-    own_c = pltpu.make_async_copy(piece(back_a, 0), piece(home_a, me), home_sem.at[0])
-    own_d = pltpu.make_async_copy(piece(back_b, 0), piece(home_b, me), home_sem.at[1])
-    own_c.start()
-    own_d.start()
-    pltpu.make_async_copy(home_a, home_a, home_sem.at[0]).wait()
-    pltpu.make_async_copy(home_b, home_b, home_sem.at[1]).wait()
-
-    moe_sum[...] = jnp.zeros_like(moe_sum)
-    over_rows = (((0,), (0,)), ((), ()))
-
-    def combine(part, _):
-        weight = gate_ref[pl.ds(part * 32, 32), :][:, None, :]
-
-        def add(wanted, values, columns):
-            exact = (choice(part, wanted) * weight).reshape(256, 128)
-            coarse = exact.astype(bf16)
-            fine = (exact - coarse.astype(f32)).astype(bf16)
-            moe_sum[:, columns] += lax.dot_general(
-                coarse, values, over_rows, preferred_element_type=f32
-            ) + lax.dot_general(fine, values, over_rows, preferred_element_type=f32)
-
-        add(slot, home_a[pl.ds(part * 256, 256), :], slice(None))
-        values = home_b[pl.ds(part * 256, 256), :]
-        add(jnp.where(slot < 4, slot + 8, 99), values, slice(0, half))
-        add(jnp.where(slot >= 4, slot + 4, 99), values, slice(half, width))
-        return 0
-
-    lax.fori_loop(0, 4, combine, 0)
-    out_ref[...] = (mid_ref[...].astype(f32) + moe_sum[...]).astype(bf16)
-    others = pl.ds(0, 127 * 8)
-    pltpu.make_async_copy(send_a.at[others], send_a.at[others], out_sem.at[0]).wait()
-    pltpu.make_async_copy(send_b.at[others], send_b.at[others], out_sem.at[1]).wait()
-    pltpu.make_async_copy(back_a.at[others], back_a.at[others], back_sem.at[0]).wait()
-    pltpu.make_async_copy(back_b.at[others], back_b.at[others], back_sem.at[1]).wait()
+        lax.fori_loop(0, count // 2, combine, 0)
+
+    rows[:512, :] = partial[...].astype(bf16)
+    for d in (1, 3, 2):
+        for p in range(3):
+            cut = part_columns(p)
+            there = on_line(p, here, d)
+            send(
+                rows.at[pl.ds(there[p] * 128, 128), cut],
+                inbox.at[here[p], :, cut],
+                sum_send.at[p],
+                sum_recv.at[p],
+                there,
+            ).start()
+    for p in range(3):
+        cut = part_columns(p)
+        arrived(inbox.at[pl.ds(0, 3), :, cut], sum_recv.at[p])
+        total = partial[pl.ds(pl.multiple_of(here[p] * 128, 128), 128), cut]
+        for d in range(1, 4):
+            total += inbox[lax.rem(here[p] + d, 4), :, cut].astype(f32)
+        out_ref[:, cut] = (mid_ref[:, cut].astype(f32) + total).astype(bf16)
+
+    for p in range(3):
+        cut = part_columns(p)
+        arrived(infos.at[p, pl.ds(0, 3)], info_send.at[p])
+        arrived(inbox.at[pl.ds(0, 3), :, cut], line_send.at[p])
+        arrived(inbox.at[pl.ds(0, 3), :, cut], sum_send.at[p])
+        for half in range(2):
+            _, count, packed, _, _ = halves[half]
+            arrived(others(packed, 4 * count, p), back_sem.at[half, p])
 
 
 def experts(moe_in, mid, ids, gates, gate_up, down):
     tokens, width = moe_in.shape
     ff = down.shape[0]
-    groups = 128 // CHUNK
+    bf16 = jnp.bfloat16
     vmem = pl.BlockSpec(memory_space=pltpu.VMEM)
     hbm = pl.BlockSpec(memory_space=pl.ANY)
-    a_shape = pltpu.VMEM((1024, width), jnp.bfloat16)
-    b_shape = pltpu.VMEM((1024, width // 2), jnp.bfloat16)
+    a_shape = pltpu.VMEM((1024, width), bf16)
+    b_shape = pltpu.VMEM((512, width), bf16)
+    three = pltpu.SemaphoreType.DMA((3,))
+    six = pltpu.SemaphoreType.DMA((2, 3))
+    info = jnp.concatenate([ids.T.astype(jnp.float32), gates.T], axis=0)
     return pl.pallas_call(
         moe_kernel,
-        out_shape=jax.ShapeDtypeStruct((tokens, width), jnp.bfloat16),
-        in_specs=[vmem] * 4 + [hbm] * 2,
+        out_shape=jax.ShapeDtypeStruct((tokens, width), bf16),
+        in_specs=[vmem] * 3 + [hbm] * 2,
         out_specs=vmem,
         scratch_shapes=[
+            pltpu.VMEM((4, tokens, width), bf16),
+            pltpu.VMEM((3, 4, 16, tokens), jnp.float32),
             a_shape,
             b_shape,
             a_shape,
@@ -301,29 +418,33 @@
             a_shape,
             b_shape,
             a_shape,
-            b_shape,
-            pltpu.VMEM((tokens, width), jnp.float32),
-            pltpu.VMEM((width, 2 * ff), jnp.bfloat16),
-            pltpu.VMEM((ff, width), jnp.bfloat16),
-            pltpu.VMEM((CHUNK * 12, width), jnp.bfloat16),
-            pltpu.VMEM((CHUNK * 12, ff), jnp.bfloat16),
-            pltpu.VMEM((CHUNK * 12, width), jnp.bfloat16),
-            pltpu.VMEM((128, 128), jnp.float32),
-            pltpu.VMEM((128, 128), jnp.float32),
+            pltpu.VMEM((1024, ff), bf16),
+            pltpu.VMEM((1024, PARTS[3] - PARTS[1]), bf16),
+            pltpu.VMEM((512, width), jnp.float32),
+            pltpu.VMEM((4, tokens, width), bf16),
+            pltpu.VMEM((3, 32, 512), jnp.float32),
+            pltpu.VMEM((3, 32, 512), jnp.float32),
+            pltpu.VMEM((width, 2 * ff), bf16),
+            pltpu.VMEM((ff, width), bf16),
             pltpu.SemaphoreType.DMA((2,)),
-            pltpu.SemaphoreType.DMA((2,)),
-            pltpu.SemaphoreType.DMA((groups,)),
-            pltpu.SemaphoreType.DMA((groups,)),
-            pltpu.SemaphoreType.DMA((2,)),
-            pltpu.SemaphoreType.DMA((2,)),
+            three,
+            three,
+            three,
+            three,
+            six,
+            six,
+            six,
+            six,
+            three,
+            three,
         ],
         compiler_params=pltpu.CompilerParams(
-            collective_id=3, has_side_effects=True, vmem_limit_bytes=60 * 1024 * 1024
+            collective_id=3, has_side_effects=True, vmem_limit_bytes=63 * 1024 * 1024
         ),
         cost_estimate=pl.CostEstimate(
             flops=20_000_000_000, bytes_accessed=400_000_000, transcendentals=1_000_000
         ),
-    )(moe_in, mid, ids.T, gates.T, gate_up, down)
+    )(moe_in, mid, info, gate_up, down)
 
 
 def arrived(ref, sem):

time: 308 us -> 276 us (0.90)
  Pallas kernels: 298 us -> 269 us
    pallas_call x1, Pallas kernels: 181 us -> 152 us  [experts(): pl.pallas_call(moe_kernel, out_shape=jax.ShapeDtypeStruct((tokens, width)...]
where the time goes in v4:
time: 276 us; the launch traced here: 275 us
  Pallas kernels  269 us (97%)
  local copies, waits for them, and re-layouts  5 us (2%)
    pallas_call x1, Pallas kernels, experts(): pl.pallas_call(moe_kernel, out_shape=jax.ShapeDtypeStruct((tokens, width)...  152 us
    pallas_call x1, Pallas kernels, front(): pl.pallas_call(front_kernel, out_shape=(jax.ShapeDtypeStruct((2, 8 * toke...  100 us
    pallas_call x1, Pallas kernels, attention(): pl.pallas_call(attention_kernel, out_shape=(row, row), in_specs=[smem] *...  16.6 us

profile of v4, /device:TPU:1, one launch (start us, length us, event | category | flops | bytes accessed | tf_op | source)
XLA Modules:
  0.0 275.4 jit_solution(3523111838918772983)
XLA Ops:
  0.6 2.4 copy.19
  3.1 0.6 maximum_bitcast_fusion.freq_ref
  3.7 100.2 %shard_map.158 = (bf16[2,1024,128]{2,1,0:T(8,128)(2,1)}, bf16[4,2,4,128,512]{4,3,2,1,0:T(8,128)(2,1)}, bf16[128,512]{1,0:T(8,128)(2,1)}, bf16[4,2,4,64,2048]{4,3...) custom-call(s32[4,4]{1,0:T(4,128)} %lengths_ref.3, bf16[128,2048]{1,0:T(8,128)(2,1)} %hidden_ref.3, f32[1,2048]{1,0:T(1,128)} %bitcast.20, ...), custom_call_target="tpu_custom_call" | custom-call | flops 1400000000 | bytes 200000000 | tf_op jit(solution)/shard_map/pallas_call | solution.py:799
  103.9 0.0 copy-start.1
  103.9 0.0 copy-start.2
  103.9 16.6 %shard_map.159 = (bf16[128,2048]{1,0:T(8,128)(2,1)}, bf16[128,2048]{1,0:T(8,128)(2,1)}) custom-call(s32[32]{0:T(128)} %table.1, s32[4,4]{1,0:T(4,128)} %lengths_ref.3, s32[4,4]{1,0:T(4,128)} %groups_ref.1, bf16[2,1024,128]{2,1,0:T(8,128)(2,1)} %get-tuple-element.9.q_ref, bf16[128,2048]{1,0:T(8,128)(2,1)} %hidden_ref.3, f32[1,2048]{1,0:T(1,128)} %bitcast.21, ...), custom_call_target="tpu_custom_call" | custom-call | flops 5000000000 | bytes 10000000 | tf_op jit(solution)/shard_map/pallas_call | solution.py:986
  120.5 0.0 copy-done.1
  120.5 0.0 copy-done.2
  120.5 0.6 pad_maximum_fusion.info_ref
  121.1 0.0 copy-start
  121.1 151.8 %shard_map.160 = bf16[128,2048]{1,0:T(8,128)(2,1)} custom-call(bf16[128,2048]{1,0:T(8,128)(2,1)} %get-tuple-element.13.x_ref, bf16[128,2048]{1,0:T(8,128)(2,1)} %get-tuple-element.14.mid_ref, f32[16,128]{1,0:T(8,128)} %pad_maximum_fusion.info_ref, bf16[2048,1536]{1,0:T(8,128)(2,1)} %bitcast.18, bf16[768,2048]{1,0:T(8,128)(2,1)} %bitcast.19), custom_call_target="tpu_custom_call" | custom-call | flops 20000000000 | bytes 400000000 | tf_op jit(solution)/shard_map/pallas_call | solution.py:406
  272.9 1.9 copy.22
  274.8 0.0 copy-done
  274.8 0.7 copy.23
  (2 shorter events, 0.0 us)
Async XLA Ops:
  103.9 16.6 %copy-start.1 = (s32[128,8]{0,1:T(8,128)S(1)}, s32[128,8]{0,1:T(8,128)}, u32[]{:S(2)}) copy-start(s32[128,8]{0,1:T(8,128)} %param.28) | copy-start | bytes 12292
  103.9 16.6 %copy-start.2 = (f32[128,8]{0,1:T(8,128)S(1)}, f32[128,8]{0,1:T(8,128)}, u32[]{:S(2)}) copy-start(f32[128,8]{0,1:T(8,128)} %param.29) | copy-start | bytes 12292
  121.1 153.7 %copy-start = (bf16[128,512]{1,0:T(8,128)(2,1)S(1)}, bf16[128,512]{1,0:T(8,128)(2,1)}, u32[]{:S(2)}) copy-start(bf16[128,512]{1,0:T(8,128)(2,1)} %get-tuple-element.19) | copy-start | bytes 393220

commit v5 on v4

--- a/solution.py
+++ b/solution.py
@@ -101,7 +101,6 @@
     home_b,
     rows,
     acts,
-    result,
     partial,
     inbox,
     ranks,
@@ -180,18 +179,12 @@
                 named += jnp.where(hit, 1.0, 0.0)
                 gate += jnp.where(hit, infos[p, q, 8 + k : 9 + k, :], 0.0)
             rank = jnp.dot(named.astype(bf16), before, preferred_element_type=f32)
-            ranks[p, :, q * 128 : (q + 1) * 128] = jnp.where(named > 0.5, rank, 99.0)
-            gates[p, :, q * 128 : (q + 1) * 128] = gate
-
-    quarter = lax.div(lax.broadcasted_iota(jnp.int32, (1, 512), 1), 128).astype(f32)
-
-    def choice(p, group, low, count):
-        many = 256 // (4 * count)
-        rank = ranks[p, pl.ds(group * many, many), :]
-        rank = jnp.where(
-            (rank >= low) & (rank < low + count), rank - low + count * quarter, -1.0
-        )
-        wanted = lax.broadcasted_iota(jnp.int32, (many, 4 * count, 512), 1).astype(f32)
+            ranks[p, q] = jnp.where(named > 0.5, rank, 99.0)
+            gates[p, q] = gate
+
+    def choice(p, q, low, count):
+        rank = ranks[p, q]
+        wanted = (low + lax.broadcasted_iota(jnp.int32, (32, count, 128), 1)).astype(f32)
         return jnp.where(rank[:, None, :] == wanted, 1.0, 0.0)
 
     halves = ((0, 8, pack_a, recv_a, home_a), (8, 4, pack_b, recv_b, home_b))
@@ -199,22 +192,28 @@
     def pack(half):
         low, count, packed, _, _ = halves[half]
 
-        def body(group, _):
+        def body(q, _):
             for p in range(3):
                 cut = part_columns(p)
-                chosen = choice(p, group, low, count).reshape(256, 512).astype(bf16)
-                values = line[:, :, cut].reshape(512, cut.stop - cut.start)
-                packed[pl.ds(group * 256, 256), cut] = jnp.dot(
-                    chosen, values, preferred_element_type=f32
-                ).astype(bf16)
+                chosen = choice(p, q, low, count).reshape(32 * count, 128).astype(bf16)
+                value = jnp.dot(chosen, line[q, :, cut], preferred_element_type=f32)
+                packed[q, :, :, cut] = value.astype(bf16).reshape(32, count, cut.stop - cut.start)
             return 0
 
-        lax.fori_loop(0, count // 2, body, 0)
-
-    def block(ref, index, size, p):
-        return ref.at[pl.ds(index * size, size), part_columns(p)]
-
-    def exchange(src, dst, size, send_sem, recv_sem):
+        lax.fori_loop(0, 4, body, 0)
+
+    def bundle(ref, a, b, core, p):
+        return ref.at[:, core * 16 + a * 4 + b, :, part_columns(p)]
+
+    def spread(ref, p, x, y, z, core):
+        cut = part_columns(p)
+        if p == 0:
+            return ref.at[:, core, y, z, :, cut]
+        if p == 1:
+            return ref.at[x, core, :, z, :, cut]
+        return ref.at[x, core, y, :, :, cut]
+
+    def visit(step):
         sign = 1 - 2 * c
 
         def body(k, _):
@@ -224,21 +223,45 @@
                 to_a = lax.rem(a + sign * lax.rem(lax.div(o, 4), 4) + 4, 4)
                 to_b = lax.rem(b + sign * lax.rem(o, 4) + 4, 4)
                 to_c = lax.rem(c + lax.div(o, 16), 2)
-                send(
-                    block(src, to_c * 16 + to_a * 4 + to_b, size, p),
-                    block(dst, c * 16 + a * 4 + b, size, p),
-                    send_sem.at[p],
-                    recv_sem.at[p],
-                    at_plane(p, here, to_a, to_b, to_c),
-                ).start()
+                step(p, to_a, to_b, to_c)
             return 0
 
         lax.fori_loop(1, 32, body, 0)
+
+    def dispatch(src, dst, send_sem, recv_sem):
+        def step(p, a, b, core):
+            send(
+                bundle(src, a, b, core, p),
+                spread(dst, p, *here),
+                send_sem.at[p],
+                recv_sem.at[p],
+                at_plane(p, here, a, b, core),
+            ).start()
+
+        visit(step)
         for p in range(3):
             a, b = in_plane(p, here)
-            index = c * 16 + a * 4 + b
             pltpu.make_async_copy(
-                block(src, index, size, p), block(dst, index, size, p), recv_sem.at[p]
+                bundle(src, a, b, c, p), spread(dst, p, *here), recv_sem.at[p]
+            ).start()
+
+    def give_back(src, dst, send_sem, recv_sem):
+        def step(p, a, b, core):
+            own_a, own_b = in_plane(p, here)
+            there = at_plane(p, here, a, b, core)
+            send(
+                spread(src, p, *there),
+                bundle(dst, own_a, own_b, c, p),
+                send_sem.at[p],
+                recv_sem.at[p],
+                there,
+            ).start()
+
+        visit(step)
+        for p in range(3):
+            a, b = in_plane(p, here)
+            pltpu.make_async_copy(
+                spread(src, p, *here), bundle(dst, a, b, c, p), recv_sem.at[p]
             ).start()
 
     for p in range(3):
@@ -247,51 +270,20 @@
     for half in range(2):
         low, count, packed, received, _ = halves[half]
         pack(half)
-        exchange(packed, received, 4 * count, out_sem.at[half], in_sem.at[half])
+        dispatch(packed, received, out_sem.at[half], in_sem.at[half])
     load_gate_up.wait()
     load_down.wait()
 
-    def swapped(count):
-        size = 16 * count
-        row = lax.broadcasted_iota(jnp.int32, (size, size), 0)
-        column = lax.broadcasted_iota(jnp.int32, (size, size), 1)
-        source = (
-            lax.rem(lax.div(row, count), 4) * 4 * count
-            + lax.div(row, 4 * count) * count
-            + lax.rem(row, count)
-        )
-        return jnp.where(column == source, 1.0, 0.0).astype(bf16)
-
-    def others(ref, size, p):
-        return ref.at[pl.ds(0, 31 * size), part_columns(p)]
+    def others(ref, p):
+        return ref.at[:, pl.ds(0, 31), :, part_columns(p)]
 
     for half in range(2):
         low, count, packed, received, home = halves[half]
-        size = 4 * count
-        total = 32 * size
+        total = 128 * count
         for p in range(3):
-            arrived(received.at[:, part_columns(p)], in_sem.at[half, p])
-        turn = swapped(count)
-        rows[:total, part_columns(0)] = received[:, part_columns(0)]
-
-        def unpack(group, _):
-            core, a = lax.div(group, 4), lax.rem(group, 4)
-            cut = part_columns(1)
-            block_y = jnp.dot(
-                turn, received[pl.ds(group * 4 * size, 4 * size), cut], preferred_element_type=f32
-            ).astype(bf16)
-            for y in range(4):
-                at = (core * 16 + y * 4 + a) * size
-                rows[pl.ds(pl.multiple_of(at, size), size), cut] = block_y[
-                    y * size : (y + 1) * size
-                ]
-            cut = part_columns(2)
-            rows[pl.ds(group * 4 * size, 4 * size), cut] = jnp.dot(
-                turn, received[pl.ds(group * 4 * size, 4 * size), cut], preferred_element_type=f32
-            ).astype(bf16)
-            return 0
-
-        lax.fori_loop(0, 8, unpack, 0)
+            whole = packed.at[:, :, :, part_columns(p)]
+            arrived(whole, in_sem.at[half, p])
+        rows[:total, :] = received[...].reshape(total, rows.shape[1])
 
         def up(tile, _):
             at = pl.multiple_of(tile * 256, 256)
@@ -302,67 +294,46 @@
             return 0
 
         lax.fori_loop(0, ff // 256, up, 0)
-        for p in range(3):
-            arrived(others(packed, size, p), out_sem.at[half, p])
-
-        def lower(group, _):
-            at = pl.multiple_of(group * 256, 256)
-            for p in range(3):
-                cut = part_columns(p)
-                value = jnp.dot(
-                    acts[pl.ds(at, 256), :], down[:, cut], preferred_element_type=f32
-                ).astype(bf16)
-                if p == 0:
-                    packed[pl.ds(at, 256), cut] = value
-                else:
-                    result[pl.ds(at, 256), cut.start - PARTS[1] : cut.stop - PARTS[1]] = value
+
+        def lower(tile, _):
+            at = pl.multiple_of(tile * 256, 256)
+            value = jnp.dot(
+                acts[:total, :], down[:, pl.ds(at, 256)], preferred_element_type=f32
+            ).astype(bf16)
+            received[:, :, :, :, :, pl.ds(at, 256)] = value.reshape(4, 2, 4, 4, count, 256)
             return 0
 
-        lax.fori_loop(0, total // 256, lower, 0)
-
-        def repack(group, _):
-            core, a = lax.div(group, 4), lax.rem(group, 4)
-            cut = slice(0, PARTS[2] - PARTS[1])
-            pieces = []
-            for y in range(4):
-                at = (core * 16 + y * 4 + a) * size
-                pieces.append(result[pl.ds(pl.multiple_of(at, size), size), cut])
-            packed[pl.ds(group * 4 * size, 4 * size), part_columns(1)] = jnp.dot(
-                turn, jnp.concatenate(pieces, axis=0), preferred_element_type=f32
-            ).astype(bf16)
-            cut = slice(PARTS[2] - PARTS[1], PARTS[3] - PARTS[1])
-            packed[pl.ds(group * 4 * size, 4 * size), part_columns(2)] = jnp.dot(
-                turn, result[pl.ds(group * 4 * size, 4 * size), cut], preferred_element_type=f32
-            ).astype(bf16)
-            return 0
-
-        lax.fori_loop(0, 8, repack, 0)
-        exchange(packed, home, size, back_sem.at[half], home_sem.at[half])
-
-    partial[...] = jnp.zeros_like(partial)
+        lax.fori_loop(0, rows.shape[1] // 256, lower, 0)
+        give_back(received, home, back_sem.at[half], home_sem.at[half])
+
     over_rows = (((0,), (0,)), ((), ()))
     for half in range(2):
         low, count, packed, received, home = halves[half]
-        many = 256 // (4 * count)
         for p in range(3):
-            arrived(home.at[:, part_columns(p)], home_sem.at[half, p])
-
-        def combine(group, _):
+            arrived(home.at[:, :, :, part_columns(p)], home_sem.at[half, p])
+
+        def combine(q, _):
+            at = pl.ds(pl.multiple_of(q * 128, 128), 128)
             for p in range(3):
                 cut = part_columns(p)
-                gate = gates[p, pl.ds(group * many, many), :]
-                exact = (choice(p, group, low, count) * gate[:, None, :]).reshape(256, 512)
+                exact = choice(p, q, low, count) * gates[p, q][:, None, :]
+                exact = exact.reshape(32 * count, 128)
                 coarse = exact.astype(bf16)
                 fine = (exact - coarse.astype(f32)).astype(bf16)
-                values = home[pl.ds(group * 256, 256), cut]
-                partial[:, cut] += lax.dot_general(
+                values = home[q, :, :, cut].reshape(32 * count, cut.stop - cut.start)
+                value = lax.dot_general(
                     coarse, values, over_rows, preferred_element_type=f32
                 ) + lax.dot_general(fine, values, over_rows, preferred_element_type=f32)
+                if half == 0:
+                    partial[at, cut] = value
+                else:
+                    value += partial[at, cut]
+                    partial[at, cut] = value
+                    rows[at, cut] = value.astype(bf16)
             return 0
 
-        lax.fori_loop(0, count // 2, combine, 0)
-
-    rows[:512, :] = partial[...].astype(bf16)
+        lax.fori_loop(0, 4, combine, 0)
+
     for d in (1, 3, 2):
         for p in range(3):
             cut = part_columns(p)
@@ -388,8 +359,8 @@
         arrived(inbox.at[pl.ds(0, 3), :, cut], line_send.at[p])
         arrived(inbox.at[pl.ds(0, 3), :, cut], sum_send.at[p])
         for half in range(2):
-            _, count, packed, _, _ = halves[half]
-            arrived(others(packed, 4 * count, p), back_sem.at[half, p])
+            arrived(others(halves[half][2], p), out_sem.at[half, p])
+            arrived(others(halves[half][2], p), back_sem.at[half, p])
 
 
 def experts(moe_in, mid, ids, gates, gate_up, down):
@@ -398,8 +369,8 @@
     bf16 = jnp.bfloat16
     vmem = pl.BlockSpec(memory_space=pltpu.VMEM)
     hbm = pl.BlockSpec(memory_space=pl.ANY)
-    a_shape = pltpu.VMEM((1024, width), bf16)
-    b_shape = pltpu.VMEM((512, width), bf16)
+    flat_a, flat_b = (pltpu.VMEM((4, 32, n, width), bf16) for n in (8, 4))
+    wide_a, wide_b = (pltpu.VMEM((4, 2, 4, 4, n, width), bf16) for n in (8, 4))
     three = pltpu.SemaphoreType.DMA((3,))
     six = pltpu.SemaphoreType.DMA((2, 3))
     info = jnp.concatenate([ids.T.astype(jnp.float32), gates.T], axis=0)
@@ -411,19 +382,18 @@
         scratch_shapes=[
             pltpu.VMEM((4, tokens, width), bf16),
             pltpu.VMEM((3, 4, 16, tokens), jnp.float32),
-            a_shape,
-            b_shape,
-            a_shape,
-            b_shape,
-            a_shape,
-            b_shape,
-            a_shape,
+            flat_a,
+            flat_b,
+            wide_a,
+            wide_b,
+            flat_a,
+            flat_b,
+            pltpu.VMEM((1024, width), bf16),
             pltpu.VMEM((1024, ff), bf16),
-            pltpu.VMEM((1024, PARTS[3] - PARTS[1]), bf16),
             pltpu.VMEM((512, width), jnp.float32),
             pltpu.VMEM((4, tokens, width), bf16),
-            pltpu.VMEM((3, 32, 512), jnp.float32),
-            pltpu.VMEM((3, 32, 512), jnp.float32),
+            pltpu.VMEM((3, 4, 32, tokens), jnp.float32),
+            pltpu.VMEM((3, 4, 32, tokens), jnp.float32),
             pltpu.VMEM((width, 2 * ff), bf16),
             pltpu.VMEM((ff, width), bf16),
             pltpu.SemaphoreType.DMA((2,)),

time: 276 us -> 270 us (0.978)
  Pallas kernels: 269 us -> 262 us
    pallas_call x1, Pallas kernels: 152 us -> 146 us  [experts(): pl.pallas_call(moe_kernel, out_shape=jax.ShapeDtypeStruct((tokens, width)...]
where the time goes in v5:
time: 270 us; the launch traced here: 269 us
  Pallas kernels  262 us (97%)
  local copies, waits for them, and re-layouts  5 us (2%)
    pallas_call x1, Pallas kernels, experts(): pl.pallas_call(moe_kernel, out_shape=jax.ShapeDtypeStruct((tokens, width)...  146 us
    pallas_call x1, Pallas kernels, front(): pl.pallas_call(front_kernel, out_shape=(jax.ShapeDtypeStruct((2, 8 * toke...  100 us
    pallas_call x1, Pallas kernels, attention(): pl.pallas_call(attention_kernel, out_shape=(row, row), in_specs=[smem] *...  16.6 us

profile of v5, /device:TPU:1, one launch (start us, length us, event | category | flops | bytes accessed | tf_op | source)
XLA Modules:
  0.0 269.2 jit_solution(9861523662544539794)
XLA Ops:
  0.6 2.4 copy.19
  3.1 0.6 maximum_bitcast_fusion.freq_ref
  3.7 100.2 %shard_map.158 = (bf16[2,1024,128]{2,1,0:T(8,128)(2,1)}, bf16[4,2,4,128,512]{4,3,2,1,0:T(8,128)(2,1)}, bf16[128,512]{1,0:T(8,128)(2,1)}, bf16[4,2,4,64,2048]{4,3...) custom-call(s32[4,4]{1,0:T(4,128)} %lengths_ref.3, bf16[128,2048]{1,0:T(8,128)(2,1)} %hidden_ref.3, f32[1,2048]{1,0:T(1,128)} %bitcast.20, ...), custom_call_target="tpu_custom_call" | custom-call | flops 1400000000 | bytes 200000000 | tf_op jit(solution)/shard_map/pallas_call | solution.py:769
  103.9 0.0 copy-start.1
  103.9 0.0 copy-start.2
  103.9 16.6 %shard_map.159 = (bf16[128,2048]{1,0:T(8,128)(2,1)}, bf16[128,2048]{1,0:T(8,128)(2,1)}) custom-call(s32[32]{0:T(128)} %table.1, s32[4,4]{1,0:T(4,128)} %lengths_ref.3, s32[4,4]{1,0:T(4,128)} %groups_ref.1, bf16[2,1024,128]{2,1,0:T(8,128)(2,1)} %get-tuple-element.9.q_ref, bf16[128,2048]{1,0:T(8,128)(2,1)} %hidden_ref.3, f32[1,2048]{1,0:T(1,128)} %bitcast.21, ...), custom_call_target="tpu_custom_call" | custom-call | flops 5000000000 | bytes 10000000 | tf_op jit(solution)/shard_map/pallas_call | solution.py:956
  120.5 0.0 copy-done.1
  120.5 0.0 copy-done.2
  120.5 0.6 pad_maximum_fusion.info_ref
  121.1 0.0 copy-start
  121.1 145.6 %shard_map.160 = bf16[128,2048]{1,0:T(8,128)(2,1)} custom-call(bf16[128,2048]{1,0:T(8,128)(2,1)} %get-tuple-element.13.x_ref, bf16[128,2048]{1,0:T(8,128)(2,1)} %get-tuple-element.14.mid_ref, f32[16,128]{1,0:T(8,128)} %pad_maximum_fusion.info_ref, bf16[2048,1536]{1,0:T(8,128)(2,1)} %bitcast.18, bf16[768,2048]{1,0:T(8,128)(2,1)} %bitcast.19), custom_call_target="tpu_custom_call" | custom-call | flops 20000000000 | bytes 400000000 | tf_op jit(solution)/shard_map/pallas_call | solution.py:377
  266.7 1.9 copy.22
  268.6 0.0 copy-done
  268.6 0.7 copy.23
  (2 shorter events, 0.0 us)
Async XLA Ops:
  103.9 16.6 %copy-start.1 = (s32[128,8]{0,1:T(8,128)S(1)}, s32[128,8]{0,1:T(8,128)}, u32[]{:S(2)}) copy-start(s32[128,8]{0,1:T(8,128)} %param.28) | copy-start | bytes 12292
  103.9 16.6 %copy-start.2 = (f32[128,8]{0,1:T(8,128)S(1)}, f32[128,8]{0,1:T(8,128)}, u32[]{:S(2)}) copy-start(f32[128,8]{0,1:T(8,128)} %param.29) | copy-start | bytes 12292
  121.1 147.5 %copy-start = (bf16[128,512]{1,0:T(8,128)(2,1)S(1)}, bf16[128,512]{1,0:T(8,128)(2,1)}, u32[]{:S(2)}) copy-start(bf16[128,512]{1,0:T(8,128)(2,1)} %get-tuple-element.19) | copy-start | bytes 393220

commit v6 on v5

--- a/solution.py
+++ b/solution.py
@@ -16,7 +16,7 @@
 
 
 MESH_ID = pl.DeviceIdType.MESH
-STEP = 45
+STEP = 1
 PARTS = (0, 640, 1280, 2048)
 
 
@@ -312,9 +312,10 @@
         for p in range(3):
             arrived(home.at[:, :, :, part_columns(p)], home_sem.at[half, p])
 
-        def combine(q, _):
-            at = pl.ds(pl.multiple_of(q * 128, 128), 128)
+        def combine(d, _):
             for p in range(3):
+                q = lax.rem(here[p] + d, 4)
+                at = pl.ds(pl.multiple_of(q * 128, 128), 128)
                 cut = part_columns(p)
                 exact = choice(p, q, low, count) * gates[p, q][:, None, :]
                 exact = exact.reshape(32 * count, 128)
@@ -330,21 +331,25 @@
                     value += partial[at, cut]
                     partial[at, cut] = value
                     rows[at, cut] = value.astype(bf16)
+            if half == 1:
+
+                @pl.when(d < 4)
+                def _():
+                    for p in range(3):
+                        cut = part_columns(p)
+                        there = on_line(p, here, d)
+                        send(
+                            rows.at[pl.ds(pl.multiple_of(there[p] * 128, 128), 128), cut],
+                            inbox.at[here[p], :, cut],
+                            sum_send.at[p],
+                            sum_recv.at[p],
+                            there,
+                        ).start()
+
             return 0
 
-        lax.fori_loop(0, 4, combine, 0)
-
-    for d in (1, 3, 2):
-        for p in range(3):
-            cut = part_columns(p)
-            there = on_line(p, here, d)
-            send(
-                rows.at[pl.ds(there[p] * 128, 128), cut],
-                inbox.at[here[p], :, cut],
-                sum_send.at[p],
-                sum_recv.at[p],
-                there,
-            ).start()
+        lax.fori_loop(1, 5, combine, 0)
+
     for p in range(3):
         cut = part_columns(p)
         arrived(inbox.at[pl.ds(0, 3), :, cut], sum_recv.at[p])
@@ -675,7 +680,6 @@
     gather.rest(1, lambda r, d, h, piece: w_pair(r, d * 2 + h, piece))
     project_out.first()
     project_out.push(1, 0)
-    project_out.push(1, 1)
     for copy in w_kept:
         copy.wait_recv()
     swap_near(project_out, w_out_ref, o_pair)
@@ -738,6 +742,7 @@
     spread.first()
     spread.push(1, 0)
     spread.push(1, 1)
+    project_out.push(1, 1)
     arrived(pages_ref.at[pl.ds(0, few)], pool_sems.at[1, 0])
     arrived(pages_ref.at[pl.ds(0, few)], pool_sems.at[1, 1])
     pool_copies.append(pool_send(3, far_row * held, held, partner))

time: 270 us -> 273 us (1.011)
  Pallas kernels: 262 us -> 266 us
where the time goes in v6:
time: 273 us
  Pallas kernels  266 us (97%)
  local copies, waits for them, and re-layouts  5 us (2%)
    pallas_call x1, Pallas kernels, experts(): pl.pallas_call(moe_kernel, out_shape=jax.ShapeDtypeStruct((tokens, width)...  148 us
    pallas_call x1, Pallas kernels, front(): pl.pallas_call(front_kernel, out_shape=(jax.ShapeDtypeStruct((2, 8 * toke...  101 us
    pallas_call x1, Pallas kernels, attention(): pl.pallas_call(attention_kernel, out_shape=(row, row), in_specs=[smem] *...  16.6 us

profile of v6, /device:TPU:1, one launch (start us, length us, event | category | flops | bytes accessed | tf_op | source)
XLA Modules:
  0.0 272.7 jit_solution(13689888301663866670)
XLA Ops:
  0.6 2.4 copy.19
  3.1 0.6 maximum_bitcast_fusion.freq_ref
  3.7 101.2 %shard_map.158 = (bf16[2,1024,128]{2,1,0:T(8,128)(2,1)}, bf16[4,2,4,128,512]{4,3,2,1,0:T(8,128)(2,1)}, bf16[128,512]{1,0:T(8,128)(2,1)}, bf16[4,2,4,64,2048]{4,3...) custom-call(s32[4,4]{1,0:T(4,128)} %lengths_ref.3, bf16[128,2048]{1,0:T(8,128)(2,1)} %hidden_ref.3, f32[1,2048]{1,0:T(1,128)} %bitcast.20, ...), custom_call_target="tpu_custom_call" | custom-call | flops 1400000000 | bytes 200000000 | tf_op jit(solution)/shard_map/pallas_call | solution.py:774
  104.9 0.0 copy-start.1
  104.9 0.0 copy-start.2
  104.9 16.6 %shard_map.159 = (bf16[128,2048]{1,0:T(8,128)(2,1)}, bf16[128,2048]{1,0:T(8,128)(2,1)}) custom-call(s32[32]{0:T(128)} %table.1, s32[4,4]{1,0:T(4,128)} %lengths_ref.3, s32[4,4]{1,0:T(4,128)} %groups_ref.1, bf16[2,1024,128]{2,1,0:T(8,128)(2,1)} %get-tuple-element.9.q_ref, bf16[128,2048]{1,0:T(8,128)(2,1)} %hidden_ref.3, f32[1,2048]{1,0:T(1,128)} %bitcast.21, ...), custom_call_target="tpu_custom_call" | custom-call | flops 5000000000 | bytes 10000000 | tf_op jit(solution)/shard_map/pallas_call | solution.py:961
  121.5 0.0 copy-done.1
  121.5 0.0 copy-done.2
  121.6 0.6 pad_maximum_fusion.info_ref
  122.2 0.0 copy-start
  122.2 147.9 %shard_map.160 = bf16[128,2048]{1,0:T(8,128)(2,1)} custom-call(bf16[128,2048]{1,0:T(8,128)(2,1)} %get-tuple-element.13.x_ref, bf16[128,2048]{1,0:T(8,128)(2,1)} %get-tuple-element.14.mid_ref, f32[16,128]{1,0:T(8,128)} %pad_maximum_fusion.info_ref, bf16[2048,1536]{1,0:T(8,128)(2,1)} %bitcast.18, bf16[768,2048]{1,0:T(8,128)(2,1)} %bitcast.19), custom_call_target="tpu_custom_call" | custom-call | flops 20000000000 | bytes 400000000 | tf_op jit(solution)/shard_map/pallas_call | solution.py:382
  270.1 1.9 copy.22
  272.0 0.0 copy-done
  272.0 0.7 copy.23
  (2 shorter events, 0.0 us)
Async XLA Ops:
  104.9 16.6 %copy-start.1 = (s32[128,8]{0,1:T(8,128)S(1)}, s32[128,8]{0,1:T(8,128)}, u32[]{:S(2)}) copy-start(s32[128,8]{0,1:T(8,128)} %param.28) | copy-start | bytes 12292
  104.9 16.6 %copy-start.2 = (f32[128,8]{0,1:T(8,128)S(1)}, f32[128,8]{0,1:T(8,128)}, u32[]{:S(2)}) copy-start(f32[128,8]{0,1:T(8,128)} %param.29) | copy-start | bytes 12292
  122.2 149.8 %copy-start = (bf16[128,512]{1,0:T(8,128)(2,1)S(1)}, bf16[128,512]{1,0:T(8,128)(2,1)}, u32[]{:S(2)}) copy-start(bf16[128,512]{1,0:T(8,128)(2,1)} %get-tuple-element.19) | copy-start | bytes 393220
